TPU v7x, 512 devices: a whole 4x4x16 slice. The times are simulated.
512 devices in a mesh: ctx: 64 (over x, y, z_hi, core), head: 8 (over z_lo).
Axes of the slice: x: 4, y: 4, z: 16 (z_hi: 2, z_lo: 8; z = z_hi * 8 + z_lo), core: 2. Of those that a mesh axis runs over, the one named last changes fastest.
Arguments:
- queries: bfloat16 [8192, 8192], P('ctx', 'head'), parts along dimension 1, may hold values from -12 to 12
- key_rows: bfloat16 [8192, 1024], P('ctx', 'head'), parts along dimension 1, may hold values from -6 to 6
- value_rows: bfloat16 [8192, 1024], P('ctx', 'head'), parts along dimension 1, may hold values from -6 to 6
- out_grad: bfloat16 [8192, 8192], P('ctx', 'head'), parts along dimension 1, may hold values from -6 to 6
- doc_lengths: int32 [16], replicated, may hold values from 1 to 2048, 8192 in all
Outputs:
- attended: bfloat16 [8192, 8192], P('ctx', 'head'), parts along dimension 1
- query_grad: bfloat16 [8192, 8192], P('ctx', 'head'), parts along dimension 1
- key_grad: bfloat16 [8192, 1024], P('ctx', 'head'), parts along dimension 1
- value_grad: bfloat16 [8192, 1024], P('ctx', 'head'), parts along dimension 1
There are 8 independent parts, one for each index of `head`. A program takes and returns all parts, laid end to end along the dimension named above; an argument that names none is the same for every part. Nothing has to cross between parts.
Inputs may be any that keep to these rules, and one draw needn't show every extreme that they name: `doc_lengths`: the documents lie end to end and cover all 8192 positions.
All inputs are finite; a program needn't handle non-finite values.
Results may differ from a plain program's by a relative error of at most 0.03.
Values may be sent and summed in bfloat16 or wider, within the bound.
A program may use at most 64 MiB of HBM per device.

v0:
```python
import jax
import jax.numpy as jnp
from jax import lax
from jax.sharding import PartitionSpec as P

DOC_CAP = 2048


big_negative = -1e30


def from_behind(value, axis, steps):
    count = lax.axis_size(axis)
    leading, last = (max(0, -steps), min(count, count - steps))
    return lax.ppermute(value, axis, [(source, source + steps) for source in range(leading, last)])


def document_ids(doc_lengths, positions):
    doc_ends = jnp.cumsum(doc_lengths)
    doc_starts = doc_ends - doc_lengths
    passed = (positions[:, None] >= doc_starts[None, :]).astype(jnp.int32)
    return jnp.sum(passed, axis=1) - 1


def on_device(queries, key_rows, value_rows, out_grad, doc_lengths):
    tokens_here = queries.shape[0]
    head_width = key_rows.shape[1]
    group_heads = queries.shape[1] // head_width
    row_count = tokens_here * group_heads
    score_scale = head_width ** (-0.5)
    devices = lax.axis_size("ctx")
    device_index = lax.axis_index("ctx")
    reach_back = min(DOC_CAP // tokens_here, devices // 4)
    blocks = reach_back + 1
    key_count = blocks * tokens_here
    offsets = jnp.arange(tokens_here, dtype=jnp.int32)
    own_pos = device_index * tokens_here + offsets
    own_doc = document_ids(doc_lengths, own_pos)
    row_doc = jnp.repeat(own_doc, group_heads)
    row_pos = jnp.repeat(own_pos, group_heads)
    query_rows = queries.reshape(row_count, head_width)
    grad_rows = out_grad.reshape(row_count, head_width)
    key_value = jnp.stack([key_rows, value_rows])
    window = jnp.zeros((2, blocks, tokens_here, head_width), key_value.dtype)
    window = lax.dynamic_update_index_in_dim(window, key_value, 0, 1)

    def relay(block_index, loop_state):
        moving, window_now = loop_state
        moving = from_behind(moving, "ctx", 1)
        window_now = lax.dynamic_update_index_in_dim(window_now, moving, block_index, 1)
        return (moving, window_now)

    window = lax.fori_loop(1, blocks, relay, (key_value, window))[1]
    keys_all = window[0].reshape(key_count, head_width)
    values_all = window[1].reshape(key_count, head_width)
    key_pos = (
        (device_index - jnp.arange(blocks, dtype=jnp.int32))[:, None] * tokens_here
        + offsets[None, :]
    ).reshape(key_count)
    key_doc = document_ids(doc_lengths, key_pos)
    block_rows = min(512, row_count)
    while block_rows > 128 and block_rows * key_count > 1500000:
        block_rows = block_rows // 2
    row_blocks = row_count // block_rows

    def row_block(carry, block_index):
        key_acc, value_acc = carry
        begin = block_index * block_rows
        query_block = lax.dynamic_slice_in_dim(query_rows, begin, block_rows, 0)
        grad_block = lax.dynamic_slice_in_dim(grad_rows, begin, block_rows, 0)
        doc_block = lax.dynamic_slice_in_dim(row_doc, begin, block_rows, 0)
        pos_block = lax.dynamic_slice_in_dim(row_pos, begin, block_rows, 0)
        allowed = (doc_block[:, None] == key_doc[None, :]) & (
            pos_block[:, None] >= key_pos[None, :]
        )
        scores = (
            lax.dot_general(
                query_block, keys_all, (((1,), (1,)), ((), ())), preferred_element_type=jnp.float32
            )
            * score_scale
        )
        masked = jnp.where(allowed, scores, big_negative)
        row_max = jnp.max(masked, axis=1)
        row_sum = jnp.sum(jnp.where(allowed, jnp.exp(masked - row_max[:, None]), 0.0), axis=1)
        log_total = row_max + jnp.log(row_sum)
        probability = jnp.where(allowed, jnp.exp(scores - log_total[:, None]), 0.0)
        rounded = probability.astype(jnp.bfloat16)
        attended_block = jnp.dot(rounded, values_all, preferred_element_type=jnp.float32).astype(
            jnp.bfloat16
        )
        row_delta = jnp.sum(
            grad_block.astype(jnp.float32) * attended_block.astype(jnp.float32), axis=1
        )
        prob_grad = lax.dot_general(
            grad_block, values_all, (((1,), (1,)), ((), ())), preferred_element_type=jnp.float32
        )
        score_grad = (probability * (prob_grad - row_delta[:, None])).astype(jnp.bfloat16)
        query_block_grad = (
            jnp.dot(score_grad, keys_all, preferred_element_type=jnp.float32) * score_scale
        ).astype(jnp.bfloat16)
        key_part = (
            lax.dot_general(
                score_grad,
                query_block,
                (((0,), (0,)), ((), ())),
                preferred_element_type=jnp.float32,
            )
            * score_scale
        )
        value_part = lax.dot_general(
            rounded, grad_block, (((0,), (0,)), ((), ())), preferred_element_type=jnp.float32
        )
        return ((key_acc + key_part, value_acc + value_part), (attended_block, query_block_grad))

    start_acc = jnp.zeros((key_count, head_width), jnp.float32)
    (key_acc, value_acc), (attended_rows, query_grad_rows) = lax.scan(
        row_block, (start_acc, start_acc), jnp.arange(row_blocks, dtype=jnp.int32)
    )
    grad_parts = jnp.stack([key_acc, value_acc]).reshape(2, blocks, tokens_here, head_width)

    def giveback(loop_index, accumulated):
        incoming = from_behind(accumulated, "ctx", -1)
        return incoming + lax.dynamic_index_in_dim(
            grad_parts, reach_back - 1 - loop_index, 1, keepdims=False
        )

    summed = lax.fori_loop(0, reach_back, giveback, grad_parts[:, reach_back])
    attended = attended_rows.reshape(tokens_here, group_heads * head_width)
    query_grad = query_grad_rows.reshape(tokens_here, group_heads * head_width)
    return (attended, query_grad, summed[0].astype(jnp.bfloat16), summed[1].astype(jnp.bfloat16))


def solution(mesh):
    placed = (P("ctx", "head"), P("ctx", "head"), P("ctx", "head"), P("ctx", "head"), P())
    return jax.shard_map(
        on_device,
        mesh=mesh,
        in_specs=placed,
        out_specs=(P("ctx", "head"), P("ctx", "head"), P("ctx", "head"), P("ctx", "head")),
        check_vma=False,
    )
```

profile of v0, /device:TPU:6, one launch (start us, length us, event | category | flops | bytes accessed | tf_op | source)
XLA Modules:
  0.0 626.7 jit_solution(5118850228534501951)
XLA Ops:
  6.1 290.2 %while.47 = (s32[]{:T(128)}, bf16[2,128,128]{2,1,0:T(8,128)(2,1)S(1)}, bf16[2,17,128,128]{3,2,0,1:T(8,128)(2,1)S(1)}, s32[]{:T(128)}, s32[]{:T(128)}, /*index=5*/s32[]{:T(128)}) while((s32[]{:T(128)}, bf16[2,128,128]{2,1,0:T(8,128)(2,1)S(1)}, bf16[2,17,128,128]{3,2,0,1:T(8,128)(2,1)S(1)}, s32[]{:T(128)}, s32[]{:T(128)}, ...), condition=%wide.region_4.5_spmd, body=%wide.region_3.4_spmd.sunk | while | flops 5 | bytes 524435 | solution.py:53
  8.0 17.9 %collective-permute-done = bf16[2,128,128]{2,1,0:T(8,128)(2,1)S(1)} collective-permute-done((bf16[2,128,128]{2,1,0:T(8,128)(2,1)S(1)}, bf16[2,128,128]{2,1,0:T(8,128)(2,1)S(1)}, u32[]{:S(2)}, u32[]{:S(2)}) %collective-permute-start) | collective-permute-done | bytes 65568 | tf_op jit(solution)/shard_map/while/body/eval_jaxpr/ppermute | solution.py:15
  45.2 16.9 %collective-permute-done = bf16[2,128,128]{2,1,0:T(8,128)(2,1)S(1)} collective-permute-done((bf16[2,128,128]{2,1,0:T(8,128)(2,1)S(1)}, bf16[2,128,128]{2,1,0:T(8,128)(2,1)S(1)}, u32[]{:S(2)}, u32[]{:S(2)}) %collective-permute-start) | collective-permute-done | bytes 65568 | tf_op jit(solution)/shard_map/while/body/eval_jaxpr/ppermute | solution.py:15
  133.5 16.8 %collective-permute-done = bf16[2,128,128]{2,1,0:T(8,128)(2,1)S(1)} collective-permute-done((bf16[2,128,128]{2,1,0:T(8,128)(2,1)S(1)}, bf16[2,128,128]{2,1,0:T(8,128)(2,1)S(1)}, u32[]{:S(2)}, u32[]{:S(2)}) %collective-permute-start) | collective-permute-done | bytes 65568 | tf_op jit(solution)/shard_map/while/body/eval_jaxpr/ppermute | solution.py:15
  152.3 16.4 %collective-permute-done = bf16[2,128,128]{2,1,0:T(8,128)(2,1)S(1)} collective-permute-done((bf16[2,128,128]{2,1,0:T(8,128)(2,1)S(1)}, bf16[2,128,128]{2,1,0:T(8,128)(2,1)S(1)}, u32[]{:S(2)}, u32[]{:S(2)}) %collective-permute-start) | collective-permute-done | bytes 65568 | tf_op jit(solution)/shard_map/while/body/eval_jaxpr/ppermute | solution.py:15
  170.7 16.4 %collective-permute-done = bf16[2,128,128]{2,1,0:T(8,128)(2,1)S(1)} collective-permute-done((bf16[2,128,128]{2,1,0:T(8,128)(2,1)S(1)}, bf16[2,128,128]{2,1,0:T(8,128)(2,1)S(1)}, u32[]{:S(2)}, u32[]{:S(2)}) %collective-permute-start) | collective-permute-done | bytes 65568 | tf_op jit(solution)/shard_map/while/body/eval_jaxpr/ppermute | solution.py:15
  189.1 16.4 %collective-permute-done = bf16[2,128,128]{2,1,0:T(8,128)(2,1)S(1)} collective-permute-done((bf16[2,128,128]{2,1,0:T(8,128)(2,1)S(1)}, bf16[2,128,128]{2,1,0:T(8,128)(2,1)S(1)}, u32[]{:S(2)}, u32[]{:S(2)}) %collective-permute-start) | collective-permute-done | bytes 65568 | tf_op jit(solution)/shard_map/while/body/eval_jaxpr/ppermute | solution.py:15
  207.4 16.4 %collective-permute-done = bf16[2,128,128]{2,1,0:T(8,128)(2,1)S(1)} collective-permute-done((bf16[2,128,128]{2,1,0:T(8,128)(2,1)S(1)}, bf16[2,128,128]{2,1,0:T(8,128)(2,1)S(1)}, u32[]{:S(2)}, u32[]{:S(2)}) %collective-permute-start) | collective-permute-done | bytes 65568 | tf_op jit(solution)/shard_map/while/body/eval_jaxpr/ppermute | solution.py:15
  225.8 16.4 %collective-permute-done = bf16[2,128,128]{2,1,0:T(8,128)(2,1)S(1)} collective-permute-done((bf16[2,128,128]{2,1,0:T(8,128)(2,1)S(1)}, bf16[2,128,128]{2,1,0:T(8,128)(2,1)S(1)}, u32[]{:S(2)}, u32[]{:S(2)}) %collective-permute-start) | collective-permute-done | bytes 65568 | tf_op jit(solution)/shard_map/while/body/eval_jaxpr/ppermute | solution.py:15
  244.2 16.4 %collective-permute-done = bf16[2,128,128]{2,1,0:T(8,128)(2,1)S(1)} collective-permute-done((bf16[2,128,128]{2,1,0:T(8,128)(2,1)S(1)}, bf16[2,128,128]{2,1,0:T(8,128)(2,1)S(1)}, u32[]{:S(2)}, u32[]{:S(2)}) %collective-permute-start) | collective-permute-done | bytes 65568 | tf_op jit(solution)/shard_map/while/body/eval_jaxpr/ppermute | solution.py:15
  262.5 16.4 %collective-permute-done = bf16[2,128,128]{2,1,0:T(8,128)(2,1)S(1)} collective-permute-done((bf16[2,128,128]{2,1,0:T(8,128)(2,1)S(1)}, bf16[2,128,128]{2,1,0:T(8,128)(2,1)S(1)}, u32[]{:S(2)}, u32[]{:S(2)}) %collective-permute-start) | collective-permute-done | bytes 65568 | tf_op jit(solution)/shard_map/while/body/eval_jaxpr/ppermute | solution.py:15
  297.4 34.3 %while.49 = (s32[]{:T(128)}, f32[2176,128]{1,0:T(8,128)S(1)}, f32[2176,128]{1,0:T(8,128)S(1)}, bf16[2,512,128]{2,1,0:T(8,128)(2,1)}, bf16[2,512,128]{2,1,0:T(8,1...) while((s32[]{:T(128)}, f32[2176,128]{1,0:T(8,128)S(1)}, ...), condition=%wide.region_9.10_spmd.clone, body=%wide.region_5.9_spmd.clone.sunk | while | flops 1749894272 | bytes 75652072 | solution.py:116
  334.0 291.2 %while.48 = (s32[]{:T(128)}, f32[2,128,128]{2,1,0:T(8,128)S(1)}, f32[2,17,128,128]{3,2,0,1:T(8,128)}, s32[]{:T(128)}, s32[]{:T(128)}, /*index=5*/s32[]{:T(128)}, s32[]{:T(128)}) while((s32[]{:T(128)}, f32[2,128,128]{2,1,0:T(8,128)S(1)}, f32[2,17,128,128]{3,2,0,1:T(8,128)}, s32[]{:T(128)}, s32[]{:T(128)}, /*index=5*/s32[]{:T(128)}, ...), condition=%wide.region_11.12_spmd, body=%wide.region_10.11_spmd.sunk | while | flops 32774 | bytes 917679 | solution.py:127
  339.5 15.6 %collective-permute-start.1 = (f32[2,128,128]{2,1,0:T(8,128)S(1)}, f32[2,128,128]{2,1,0:T(8,128)S(1)}, u32[]{:S(2)}, u32[]{:S(2)}) collective-permute-start(f32[2,128,128]{2,1,0:T(8,128)S(1)} %get-tuple-element.588), channel_id=1, source_target_pairs={{8,0},{16,8},{24,16},{32,24},{40,32},{48,40},{56,48},{64,56},{72,6... | collective-permute-start | bytes 393224 | tf_op jit(solution)/shard_map/while/body/eval_jaxpr/ppermute | solution.py:15
  359.8 15.7 %collective-permute-start.1 = (f32[2,128,128]{2,1,0:T(8,128)S(1)}, f32[2,128,128]{2,1,0:T(8,128)S(1)}, u32[]{:S(2)}, u32[]{:S(2)}) collective-permute-start(f32[2,128,128]{2,1,0:T(8,128)S(1)} %get-tuple-element.588), channel_id=1, source_target_pairs={{8,0},{16,8},{24,16},{32,24},{40,32},{48,40},{56,48},{64,56},{72,6... | collective-permute-start | bytes 393224 | tf_op jit(solution)/shard_map/while/body/eval_jaxpr/ppermute | solution.py:15
  378.9 15.5 %collective-permute-start.1 = (f32[2,128,128]{2,1,0:T(8,128)S(1)}, f32[2,128,128]{2,1,0:T(8,128)S(1)}, u32[]{:S(2)}, u32[]{:S(2)}) collective-permute-start(f32[2,128,128]{2,1,0:T(8,128)S(1)} %get-tuple-element.588), channel_id=1, source_target_pairs={{8,0},{16,8},{24,16},{32,24},{40,32},{48,40},{56,48},{64,56},{72,6... | collective-permute-start | bytes 393224 | tf_op jit(solution)/shard_map/while/body/eval_jaxpr/ppermute | solution.py:15
  397.9 15.5 %collective-permute-start.1 = (f32[2,128,128]{2,1,0:T(8,128)S(1)}, f32[2,128,128]{2,1,0:T(8,128)S(1)}, u32[]{:S(2)}, u32[]{:S(2)}) collective-permute-start(f32[2,128,128]{2,1,0:T(8,128)S(1)} %get-tuple-element.588), channel_id=1, source_target_pairs={{8,0},{16,8},{24,16},{32,24},{40,32},{48,40},{56,48},{64,56},{72,6... | collective-permute-start | bytes 393224 | tf_op jit(solution)/shard_map/while/body/eval_jaxpr/ppermute | solution.py:15
  416.8 15.5 %collective-permute-start.1 = (f32[2,128,128]{2,1,0:T(8,128)S(1)}, f32[2,128,128]{2,1,0:T(8,128)S(1)}, u32[]{:S(2)}, u32[]{:S(2)}) collective-permute-start(f32[2,128,128]{2,1,0:T(8,128)S(1)} %get-tuple-element.588), channel_id=1, source_target_pairs={{8,0},{16,8},{24,16},{32,24},{40,32},{48,40},{56,48},{64,56},{72,6... | collective-permute-start | bytes 393224 | tf_op jit(solution)/shard_map/while/body/eval_jaxpr/ppermute | solution.py:15
  435.8 15.5 %collective-permute-start.1 = (f32[2,128,128]{2,1,0:T(8,128)S(1)}, f32[2,128,128]{2,1,0:T(8,128)S(1)}, u32[]{:S(2)}, u32[]{:S(2)}) collective-permute-start(f32[2,128,128]{2,1,0:T(8,128)S(1)} %get-tuple-element.588), channel_id=1, source_target_pairs={{8,0},{16,8},{24,16},{32,24},{40,32},{48,40},{56,48},{64,56},{72,6... | collective-permute-start | bytes 393224 | tf_op jit(solution)/shard_map/while/body/eval_jaxpr/ppermute | solution.py:15
  454.7 15.5 %collective-permute-start.1 = (f32[2,128,128]{2,1,0:T(8,128)S(1)}, f32[2,128,128]{2,1,0:T(8,128)S(1)}, u32[]{:S(2)}, u32[]{:S(2)}) collective-permute-start(f32[2,128,128]{2,1,0:T(8,128)S(1)} %get-tuple-element.588), channel_id=1, source_target_pairs={{8,0},{16,8},{24,16},{32,24},{40,32},{48,40},{56,48},{64,56},{72,6... | collective-permute-start | bytes 393224 | tf_op jit(solution)/shard_map/while/body/eval_jaxpr/ppermute | solution.py:15
  473.7 15.5 %collective-permute-start.1 = (f32[2,128,128]{2,1,0:T(8,128)S(1)}, f32[2,128,128]{2,1,0:T(8,128)S(1)}, u32[]{:S(2)}, u32[]{:S(2)}) collective-permute-start(f32[2,128,128]{2,1,0:T(8,128)S(1)} %get-tuple-element.588), channel_id=1, source_target_pairs={{8,0},{16,8},{24,16},{32,24},{40,32},{48,40},{56,48},{64,56},{72,6... | collective-permute-start | bytes 393224 | tf_op jit(solution)/shard_map/while/body/eval_jaxpr/ppermute | solution.py:15
  492.6 15.5 %collective-permute-start.1 = (f32[2,128,128]{2,1,0:T(8,128)S(1)}, f32[2,128,128]{2,1,0:T(8,128)S(1)}, u32[]{:S(2)}, u32[]{:S(2)}) collective-permute-start(f32[2,128,128]{2,1,0:T(8,128)S(1)} %get-tuple-element.588), channel_id=1, source_target_pairs={{8,0},{16,8},{24,16},{32,24},{40,32},{48,40},{56,48},{64,56},{72,6... | collective-permute-start | bytes 393224 | tf_op jit(solution)/shard_map/while/body/eval_jaxpr/ppermute | solution.py:15
  511.6 15.5 %collective-permute-start.1 = (f32[2,128,128]{2,1,0:T(8,128)S(1)}, f32[2,128,128]{2,1,0:T(8,128)S(1)}, u32[]{:S(2)}, u32[]{:S(2)}) collective-permute-start(f32[2,128,128]{2,1,0:T(8,128)S(1)} %get-tuple-element.588), channel_id=1, source_target_pairs={{8,0},{16,8},{24,16},{32,24},{40,32},{48,40},{56,48},{64,56},{72,6... | collective-permute-start | bytes 393224 | tf_op jit(solution)/shard_map/while/body/eval_jaxpr/ppermute | solution.py:15
  549.5 15.5 %collective-permute-start.1 = (f32[2,128,128]{2,1,0:T(8,128)S(1)}, f32[2,128,128]{2,1,0:T(8,128)S(1)}, u32[]{:S(2)}, u32[]{:S(2)}) collective-permute-start(f32[2,128,128]{2,1,0:T(8,128)S(1)} %get-tuple-element.588), channel_id=1, source_target_pairs={{8,0},{16,8},{24,16},{32,24},{40,32},{48,40},{56,48},{64,56},{72,6... | collective-permute-start | bytes 393224 | tf_op jit(solution)/shard_map/while/body/eval_jaxpr/ppermute | solution.py:15
  (182 shorter events, 286.2 us)
Async XLA Ops:
  6.1 19.9 %collective-permute-start = (bf16[2,128,128]{2,1,0:T(8,128)(2,1)S(1)}, bf16[2,128,128]{2,1,0:T(8,128)(2,1)S(1)}, u32[]{:S(2)}, u32[]{:S(2)}) collective-permute-start(bf16[2,128,128]{2,1,0:T(8,128)(2,1)S(1)} %get-tuple-element.515), channel_id=1, source_target_pairs={{0,8},{8,16},{16,24},{24,32},{32,40},{40,48},{48,56},{56,64},{64,7... | collective-permute-start | bytes 196616 | tf_op jit(solution)/shard_map/while/body/eval_jaxpr/ppermute | solution.py:15
  43.3 18.8 %collective-permute-start = (bf16[2,128,128]{2,1,0:T(8,128)(2,1)S(1)}, bf16[2,128,128]{2,1,0:T(8,128)(2,1)S(1)}, u32[]{:S(2)}, u32[]{:S(2)}) collective-permute-start(bf16[2,128,128]{2,1,0:T(8,128)(2,1)S(1)} %get-tuple-element.515), channel_id=1, source_target_pairs={{0,8},{8,16},{16,24},{24,32},{32,40},{40,48},{48,56},{56,64},{64,7... | collective-permute-start | bytes 196616 | tf_op jit(solution)/shard_map/while/body/eval_jaxpr/ppermute | solution.py:15
  131.6 18.7 %collective-permute-start = (bf16[2,128,128]{2,1,0:T(8,128)(2,1)S(1)}, bf16[2,128,128]{2,1,0:T(8,128)(2,1)S(1)}, u32[]{:S(2)}, u32[]{:S(2)}) collective-permute-start(bf16[2,128,128]{2,1,0:T(8,128)(2,1)S(1)} %get-tuple-element.515), channel_id=1, source_target_pairs={{0,8},{8,16},{16,24},{24,32},{32,40},{40,48},{48,56},{56,64},{64,7... | collective-permute-start | bytes 196616 | tf_op jit(solution)/shard_map/while/body/eval_jaxpr/ppermute | solution.py:15
  150.4 18.4 %collective-permute-start = (bf16[2,128,128]{2,1,0:T(8,128)(2,1)S(1)}, bf16[2,128,128]{2,1,0:T(8,128)(2,1)S(1)}, u32[]{:S(2)}, u32[]{:S(2)}) collective-permute-start(bf16[2,128,128]{2,1,0:T(8,128)(2,1)S(1)} %get-tuple-element.515), channel_id=1, source_target_pairs={{0,8},{8,16},{16,24},{24,32},{32,40},{40,48},{48,56},{56,64},{64,7... | collective-permute-start | bytes 196616 | tf_op jit(solution)/shard_map/while/body/eval_jaxpr/ppermute | solution.py:15
  168.8 18.4 %collective-permute-start = (bf16[2,128,128]{2,1,0:T(8,128)(2,1)S(1)}, bf16[2,128,128]{2,1,0:T(8,128)(2,1)S(1)}, u32[]{:S(2)}, u32[]{:S(2)}) collective-permute-start(bf16[2,128,128]{2,1,0:T(8,128)(2,1)S(1)} %get-tuple-element.515), channel_id=1, source_target_pairs={{0,8},{8,16},{16,24},{24,32},{32,40},{40,48},{48,56},{56,64},{64,7... | collective-permute-start | bytes 196616 | tf_op jit(solution)/shard_map/while/body/eval_jaxpr/ppermute | solution.py:15
  187.2 18.3 %collective-permute-start = (bf16[2,128,128]{2,1,0:T(8,128)(2,1)S(1)}, bf16[2,128,128]{2,1,0:T(8,128)(2,1)S(1)}, u32[]{:S(2)}, u32[]{:S(2)}) collective-permute-start(bf16[2,128,128]{2,1,0:T(8,128)(2,1)S(1)} %get-tuple-element.515), channel_id=1, source_target_pairs={{0,8},{8,16},{16,24},{24,32},{32,40},{40,48},{48,56},{56,64},{64,7... | collective-permute-start | bytes 196616 | tf_op jit(solution)/shard_map/while/body/eval_jaxpr/ppermute | solution.py:15
  205.5 18.3 %collective-permute-start = (bf16[2,128,128]{2,1,0:T(8,128)(2,1)S(1)}, bf16[2,128,128]{2,1,0:T(8,128)(2,1)S(1)}, u32[]{:S(2)}, u32[]{:S(2)}) collective-permute-start(bf16[2,128,128]{2,1,0:T(8,128)(2,1)S(1)} %get-tuple-element.515), channel_id=1, source_target_pairs={{0,8},{8,16},{16,24},{24,32},{32,40},{40,48},{48,56},{56,64},{64,7... | collective-permute-start | bytes 196616 | tf_op jit(solution)/shard_map/while/body/eval_jaxpr/ppermute | solution.py:15
  223.9 18.3 %collective-permute-start = (bf16[2,128,128]{2,1,0:T(8,128)(2,1)S(1)}, bf16[2,128,128]{2,1,0:T(8,128)(2,1)S(1)}, u32[]{:S(2)}, u32[]{:S(2)}) collective-permute-start(bf16[2,128,128]{2,1,0:T(8,128)(2,1)S(1)} %get-tuple-element.515), channel_id=1, source_target_pairs={{0,8},{8,16},{16,24},{24,32},{32,40},{40,48},{48,56},{56,64},{64,7... | collective-permute-start | bytes 196616 | tf_op jit(solution)/shard_map/while/body/eval_jaxpr/ppermute | solution.py:15
  242.2 18.3 %collective-permute-start = (bf16[2,128,128]{2,1,0:T(8,128)(2,1)S(1)}, bf16[2,128,128]{2,1,0:T(8,128)(2,1)S(1)}, u32[]{:S(2)}, u32[]{:S(2)}) collective-permute-start(bf16[2,128,128]{2,1,0:T(8,128)(2,1)S(1)} %get-tuple-element.515), channel_id=1, source_target_pairs={{0,8},{8,16},{16,24},{24,32},{32,40},{40,48},{48,56},{56,64},{64,7... | collective-permute-start | bytes 196616 | tf_op jit(solution)/shard_map/while/body/eval_jaxpr/ppermute | solution.py:15
  260.6 18.3 %collective-permute-start = (bf16[2,128,128]{2,1,0:T(8,128)(2,1)S(1)}, bf16[2,128,128]{2,1,0:T(8,128)(2,1)S(1)}, u32[]{:S(2)}, u32[]{:S(2)}) collective-permute-start(bf16[2,128,128]{2,1,0:T(8,128)(2,1)S(1)} %get-tuple-element.515), channel_id=1, source_target_pairs={{0,8},{8,16},{16,24},{24,32},{32,40},{40,48},{48,56},{56,64},{64,7... | collective-permute-start | bytes 196616 | tf_op jit(solution)/shard_map/while/body/eval_jaxpr/ppermute | solution.py:15
  339.5 19.4 %collective-permute-start.1 = (f32[2,128,128]{2,1,0:T(8,128)S(1)}, f32[2,128,128]{2,1,0:T(8,128)S(1)}, u32[]{:S(2)}, u32[]{:S(2)}) collective-permute-start(f32[2,128,128]{2,1,0:T(8,128)S(1)} %get-tuple-element.588), channel_id=1, source_target_pairs={{8,0},{16,8},{24,16},{32,24},{40,32},{48,40},{56,48},{64,56},{72,6... | collective-permute-start | bytes 393224 | tf_op jit(solution)/shard_map/while/body/eval_jaxpr/ppermute | solution.py:15
  359.8 18.2 %collective-permute-start.1 = (f32[2,128,128]{2,1,0:T(8,128)S(1)}, f32[2,128,128]{2,1,0:T(8,128)S(1)}, u32[]{:S(2)}, u32[]{:S(2)}) collective-permute-start(f32[2,128,128]{2,1,0:T(8,128)S(1)} %get-tuple-element.588), channel_id=1, source_target_pairs={{8,0},{16,8},{24,16},{32,24},{40,32},{48,40},{56,48},{64,56},{72,6... | collective-permute-start | bytes 393224 | tf_op jit(solution)/shard_map/while/body/eval_jaxpr/ppermute | solution.py:15
  378.9 18.0 %collective-permute-start.1 = (f32[2,128,128]{2,1,0:T(8,128)S(1)}, f32[2,128,128]{2,1,0:T(8,128)S(1)}, u32[]{:S(2)}, u32[]{:S(2)}) collective-permute-start(f32[2,128,128]{2,1,0:T(8,128)S(1)} %get-tuple-element.588), channel_id=1, source_target_pairs={{8,0},{16,8},{24,16},{32,24},{40,32},{48,40},{56,48},{64,56},{72,6... | collective-permute-start | bytes 393224 | tf_op jit(solution)/shard_map/while/body/eval_jaxpr/ppermute | solution.py:15
  397.9 18.0 %collective-permute-start.1 = (f32[2,128,128]{2,1,0:T(8,128)S(1)}, f32[2,128,128]{2,1,0:T(8,128)S(1)}, u32[]{:S(2)}, u32[]{:S(2)}) collective-permute-start(f32[2,128,128]{2,1,0:T(8,128)S(1)} %get-tuple-element.588), channel_id=1, source_target_pairs={{8,0},{16,8},{24,16},{32,24},{40,32},{48,40},{56,48},{64,56},{72,6... | collective-permute-start | bytes 393224 | tf_op jit(solution)/shard_map/while/body/eval_jaxpr/ppermute | solution.py:15
  416.8 18.0 %collective-permute-start.1 = (f32[2,128,128]{2,1,0:T(8,128)S(1)}, f32[2,128,128]{2,1,0:T(8,128)S(1)}, u32[]{:S(2)}, u32[]{:S(2)}) collective-permute-start(f32[2,128,128]{2,1,0:T(8,128)S(1)} %get-tuple-element.588), channel_id=1, source_target_pairs={{8,0},{16,8},{24,16},{32,24},{40,32},{48,40},{56,48},{64,56},{72,6... | collective-permute-start | bytes 393224 | tf_op jit(solution)/shard_map/while/body/eval_jaxpr/ppermute | solution.py:15
  435.8 18.0 %collective-permute-start.1 = (f32[2,128,128]{2,1,0:T(8,128)S(1)}, f32[2,128,128]{2,1,0:T(8,128)S(1)}, u32[]{:S(2)}, u32[]{:S(2)}) collective-permute-start(f32[2,128,128]{2,1,0:T(8,128)S(1)} %get-tuple-element.588), channel_id=1, source_target_pairs={{8,0},{16,8},{24,16},{32,24},{40,32},{48,40},{56,48},{64,56},{72,6... | collective-permute-start | bytes 393224 | tf_op jit(solution)/shard_map/while/body/eval_jaxpr/ppermute | solution.py:15
  454.7 18.0 %collective-permute-start.1 = (f32[2,128,128]{2,1,0:T(8,128)S(1)}, f32[2,128,128]{2,1,0:T(8,128)S(1)}, u32[]{:S(2)}, u32[]{:S(2)}) collective-permute-start(f32[2,128,128]{2,1,0:T(8,128)S(1)} %get-tuple-element.588), channel_id=1, source_target_pairs={{8,0},{16,8},{24,16},{32,24},{40,32},{48,40},{56,48},{64,56},{72,6... | collective-permute-start | bytes 393224 | tf_op jit(solution)/shard_map/while/body/eval_jaxpr/ppermute | solution.py:15
  473.7 18.0 %collective-permute-start.1 = (f32[2,128,128]{2,1,0:T(8,128)S(1)}, f32[2,128,128]{2,1,0:T(8,128)S(1)}, u32[]{:S(2)}, u32[]{:S(2)}) collective-permute-start(f32[2,128,128]{2,1,0:T(8,128)S(1)} %get-tuple-element.588), channel_id=1, source_target_pairs={{8,0},{16,8},{24,16},{32,24},{40,32},{48,40},{56,48},{64,56},{72,6... | collective-permute-start | bytes 393224 | tf_op jit(solution)/shard_map/while/body/eval_jaxpr/ppermute | solution.py:15
  492.6 18.0 %collective-permute-start.1 = (f32[2,128,128]{2,1,0:T(8,128)S(1)}, f32[2,128,128]{2,1,0:T(8,128)S(1)}, u32[]{:S(2)}, u32[]{:S(2)}) collective-permute-start(f32[2,128,128]{2,1,0:T(8,128)S(1)} %get-tuple-element.588), channel_id=1, source_target_pairs={{8,0},{16,8},{24,16},{32,24},{40,32},{48,40},{56,48},{64,56},{72,6... | collective-permute-start | bytes 393224 | tf_op jit(solution)/shard_map/while/body/eval_jaxpr/ppermute | solution.py:15
  511.6 18.0 %collective-permute-start.1 = (f32[2,128,128]{2,1,0:T(8,128)S(1)}, f32[2,128,128]{2,1,0:T(8,128)S(1)}, u32[]{:S(2)}, u32[]{:S(2)}) collective-permute-start(f32[2,128,128]{2,1,0:T(8,128)S(1)} %get-tuple-element.588), channel_id=1, source_target_pairs={{8,0},{16,8},{24,16},{32,24},{40,32},{48,40},{56,48},{64,56},{72,6... | collective-permute-start | bytes 393224 | tf_op jit(solution)/shard_map/while/body/eval_jaxpr/ppermute | solution.py:15
  530.5 18.0 %collective-permute-start.1 = (f32[2,128,128]{2,1,0:T(8,128)S(1)}, f32[2,128,128]{2,1,0:T(8,128)S(1)}, u32[]{:S(2)}, u32[]{:S(2)}) collective-permute-start(f32[2,128,128]{2,1,0:T(8,128)S(1)} %get-tuple-element.588), channel_id=1, source_target_pairs={{8,0},{16,8},{24,16},{32,24},{40,32},{48,40},{56,48},{64,56},{72,6... | collective-permute-start | bytes 393224 | tf_op jit(solution)/shard_map/while/body/eval_jaxpr/ppermute | solution.py:15
  549.5 18.0 %collective-permute-start.1 = (f32[2,128,128]{2,1,0:T(8,128)S(1)}, f32[2,128,128]{2,1,0:T(8,128)S(1)}, u32[]{:S(2)}, u32[]{:S(2)}) collective-permute-start(f32[2,128,128]{2,1,0:T(8,128)S(1)} %get-tuple-element.588), channel_id=1, source_target_pairs={{8,0},{16,8},{24,16},{32,24},{40,32},{48,40},{56,48},{64,56},{72,6... | collective-permute-start | bytes 393224 | tf_op jit(solution)/shard_map/while/body/eval_jaxpr/ppermute | solution.py:15
  568.4 18.0 %collective-permute-start.1 = (f32[2,128,128]{2,1,0:T(8,128)S(1)}, f32[2,128,128]{2,1,0:T(8,128)S(1)}, u32[]{:S(2)}, u32[]{:S(2)}) collective-permute-start(f32[2,128,128]{2,1,0:T(8,128)S(1)} %get-tuple-element.588), channel_id=1, source_target_pairs={{8,0},{16,8},{24,16},{32,24},{40,32},{48,40},{56,48},{64,56},{72,6... | collective-permute-start | bytes 393224 | tf_op jit(solution)/shard_map/while/body/eval_jaxpr/ppermute | solution.py:15
  587.3 18.0 %collective-permute-start.1 = (f32[2,128,128]{2,1,0:T(8,128)S(1)}, f32[2,128,128]{2,1,0:T(8,128)S(1)}, u32[]{:S(2)}, u32[]{:S(2)}) collective-permute-start(f32[2,128,128]{2,1,0:T(8,128)S(1)} %get-tuple-element.588), channel_id=1, source_target_pairs={{8,0},{16,8},{24,16},{32,24},{40,32},{48,40},{56,48},{64,56},{72,6... | collective-permute-start | bytes 393224 | tf_op jit(solution)/shard_map/while/body/eval_jaxpr/ppermute | solution.py:15
  (21 other events, 458.4 us)
where the time goes:
time: 633 us; the launch traced here: 627 us
  waiting for transfers between devices  300 us (47%)
  starting transfers between devices  266 us (42%)
  matrix products  25.2 us (4%)
  other arithmetic  21.7 us (3%)
  local copies, waits for them, and re-layouts  11.1 us (2%)
    ppermute x32, waiting for transfers between devices, from_behind(): lax.ppermute(value, axis, [(source, source + steps) for source in range(l...  300 us
    ppermute x32, starting transfers between devices, from_behind(): lax.ppermute(value, axis, [(source, source + steps) for source in range(l...  266 us
    add x16, other arithmetic, giveback(): incoming + lax.dynamic_index_in_dim(grad_parts, reach_back - 1 - loop_ind...  14.7 us
  transfers between devices with their start and end apart: 32, of which 32 were waited for; matrix products, arithmetic and copies ran while one was open for 0% of the time, Pallas kernels for 0%

commit v1 on v0

v1 whole, which is shorter than its diff:
```python
import functools
import math

import jax
import jax.numpy as jnp
from jax import lax
from jax.experimental import pallas as pl
from jax.experimental.pallas import tpu as pltpu
from jax.sharding import PartitionSpec as P

MESH = pl.DeviceIdType.MESH
T = 128
D = 128
G = 8
ROWS = T * G
PAIRS = 9
CHUNK = 256
NEG = -1e30
SCALE = D**-0.5
NT = (((1,), (1,)), ((), ()))
NN = (((1,), (0,)), ((), ()))
F32, BF16 = jnp.float32, jnp.bfloat16


def dot(a, b, dims):
    return lax.dot_general(a, b, dims, preferred_element_type=F32)


def kernel(
    n_ctx,
    q_hbm, k_hbm, v_hbm, g_hbm, lengths,
    att_hbm, dq_hbm, dk_hbm, dv_hbm,
    kv, qs, gs, qt, gt, sbuf, pbuf, bias, mrow, lrow, acc, att, dqo,
    part, s1, r1, s2, r2, r3, s3, r4, fin,
    ld_q, ld_g, ld_kv, st_att, st_dq, st_kv,
    z_s, own_s, rel_s, fwd_s, kr, fr, g1_s, g1_r, g2_s, g2_r, g3_r, g4_s, g4_r,
):
    c = lax.axis_index("ctx")
    z = lax.rem(c // 2, 2)
    core = lax.rem(c, 2)
    mate = c + 1 - 2 * core
    across = c + 2 - 4 * z
    low, high = pl.ds(0, T), pl.ds(T, T)

    def send(src, dst, ss, rs, dev):
        return pltpu.make_async_remote_copy(
            src_ref=src, dst_ref=dst, send_sem=ss, recv_sem=rs, device_id={"ctx": dev}, device_id_type=MESH
        )

    own_in = [
        pltpu.make_async_copy(src, kv.at[0, kind, low], ld_kv.at[kind]) for kind, src in enumerate((k_hbm, v_hbm))
    ]
    q_in = [
        pltpu.make_async_copy(q_hbm.at[:, pl.ds(h * D, D)], qs.at[pl.ds(h * T, T)], ld_q.at[h]) for h in range(G)
    ]
    g_in = [
        pltpu.make_async_copy(g_hbm.at[:, pl.ds(h * D, D)], gs.at[pl.ds(h * T, T)], ld_g.at[h]) for h in range(G)
    ]
    for copy in own_in + q_in + g_in:
        copy.start()

    def clear(i, _):
        kv[i] = jnp.zeros((2, 2 * T, D), BF16)
        return 0

    lax.fori_loop(1, PAIRS + 1, clear, 0)
    r2[...] = jnp.zeros_like(r2)
    r3[...] = jnp.zeros_like(r3)

    barrier = pltpu.get_barrier_semaphore()
    for dev in (mate, across):
        pl.semaphore_signal(barrier, inc=1, device_id={"ctx": dev}, device_id_type=MESH)
    count = 2
    for d in range(1, 5):
        up, down = c + 4 * d < n_ctx, c - 4 * d >= 0
        count = count + up.astype(jnp.int32) + down.astype(jnp.int32)

        @pl.when(up)
        def _():
            pl.semaphore_signal(barrier, inc=1, device_id={"ctx": c + 4 * d}, device_id_type=MESH)

        @pl.when(down)
        def _():
            pl.semaphore_signal(barrier, inc=1, device_id={"ctx": c - 4 * d}, device_id_type=MESH)

    for copy in own_in:
        copy.wait()
    pl.semaphore_wait(barrier, count)

    land = 1 + 8 * z
    here = 9 - 8 * z

    def z_send(kind):
        return send(kv.at[0, kind, low], kv.at[land, kind, low], z_s.at[kind], kr.at[land, kind], across)

    def own_send(d, kind):
        return send(
            kv.at[0, kind, low], kv.at[2 * d, kind, low], own_s.at[d, kind], kr.at[2 * d, kind], c + 4 * d
        )

    def relay_send(d, kind):
        to = 2 * d - 1 + 2 * z
        return send(kv.at[here, kind, low], kv.at[to, kind, low], rel_s.at[d, kind], kr.at[to, kind], c + 4 * d)

    def forward(i, kind):
        return send(kv.at[i, kind, low], kv.at[i, kind, high], fwd_s.at[i, kind], fr.at[i, kind], mate)

    def arrived(i, kind):
        return send(kv.at[i, kind, low], kv.at[i, kind, low], z_s.at[kind], kr.at[i, kind], mate)

    relays = lambda d: (c + 4 * d < n_ctx) & (2 * d - 1 + 2 * z < PAIRS)

    for kind in range(2):
        z_send(kind).start()
    for kind in range(2):
        forward(0, kind).start()
        for d in range(1, 5):

            @pl.when(c + 4 * d < n_ctx)
            def _():
                own_send(d, kind).start()

    row = c * T + lax.broadcasted_iota(jnp.int32, (T, 2 * T), 0)
    lane = lax.broadcasted_iota(jnp.int32, (T, 2 * T), 1)
    doc = jnp.zeros((T, 2 * T), jnp.int32)
    start = jnp.int32(0)
    for j in range(lengths.shape[0]):
        doc = jnp.where(row >= start, start, doc)
        start = start + lengths[j]
    first = lane + jnp.where(lane < T, c * T, mate * T - T)

    def mask(i, _):
        key = first - i * (2 * T)
        bias[i] = jnp.where((key >= doc) & (key <= row), 0.0, NEG)
        return 0

    lax.fori_loop(0, PAIRS, mask, 0)
    for copy in q_in:
        copy.wait()
    mrow[...] = jnp.full_like(mrow, NEG)

    def scores(i):
        key = kv[i, 0]
        b = bias[i]
        b = jnp.concatenate([b, b], axis=0)
        for t in range(ROWS // CHUNK):
            rows = pl.ds(t * CHUNK, CHUNK)
            s = dot(qs[rows], key, NT) + b
            sbuf[i, rows] = s
            mrow[rows] = jnp.maximum(mrow[rows], jnp.maximum(s[:, :T], s[:, T:]))

    def take(i, kind):
        @pl.when(c >= 2 * i)
        def _():
            arrived(i, kind).wait_recv()
            forward(i, kind).start()

    def near(n, _):
        i = 2 * n

        @pl.when(n < 4)
        def _():
            for kind in range(2):
                take(i + 2, kind)

        @pl.when(c >= 2 * i)
        def _():
            forward(i, 0).wait_recv()

        scores(i)
        return 0

    lax.fori_loop(0, 5, near, 0)

    for h in range(G):
        rows = pl.ds(h * T, T)
        qt[:, rows] = qs[rows].astype(F32).T.astype(BF16)

    for kind in range(2):
        arrived(here, kind).wait_recv()
        for d in range(1, 5):

            @pl.when(relays(d))
            def _():
                relay_send(d, kind).start()

    for kind in range(2):

        @pl.when(z == 1)
        def _():
            forward(1, kind).start()

        @pl.when(z == 0)
        def _():
            take(1, kind)

        for i in (3, 5, 7):
            take(i, kind)

    def far(n, _):
        i = 2 * n + 1

        @pl.when(c >= 2 * i)
        def _():
            forward(i, 0).wait_recv()

        scores(i)
        return 0

    lax.fori_loop(0, 4, far, 0)

    for t in range(ROWS // CHUNK):
        rows = pl.ds(t * CHUNK, CHUNK)
        mrow[rows] = jnp.broadcast_to(jnp.max(mrow[rows], axis=1, keepdims=True), (CHUNK, T))
    lrow[...] = jnp.zeros_like(lrow)
    acc[...] = jnp.zeros_like(acc)

    def weigh(n, _):
        i = jnp.where(n < 5, 2 * n, 2 * n - 9)

        @pl.when(c >= 2 * i)
        def _():
            forward(i, 1).wait_recv()

        value = kv[i, 1]
        for t in range(ROWS // CHUNK):
            rows = pl.ds(t * CHUNK, CHUNK)
            m = mrow[rows]
            p = jnp.exp2((sbuf[i, rows] - jnp.concatenate([m, m], axis=1)) * (SCALE * math.log2(math.e)))
            lrow[rows] += p[:, :T] + p[:, T:]
            p = p.astype(BF16)
            pbuf[i, rows] = p
            acc[rows] += dot(p, value, NN)
        return 0

    lax.fori_loop(0, PAIRS, weigh, 0)

    for copy in g_in:
        copy.wait()
    for h in range(G):
        rows = pl.ds(h * T, T)
        inverse = 1.0 / jnp.sum(lrow[rows], axis=1, keepdims=True)
        out = (acc[rows] * inverse).astype(BF16)
        att[rows] = out
        grad = (gs[rows].astype(F32) * inverse).astype(BF16)
        gs[rows] = grad
        grad = grad.astype(F32)
        gt[:, rows] = grad.T.astype(BF16)
        delta = jnp.sum(grad * out.astype(F32), axis=1, keepdims=True)
        lrow[rows] = jnp.broadcast_to(delta, (T, T))
    att_out = [
        pltpu.make_async_copy(att.at[pl.ds(h * T, T)], att_hbm.at[:, pl.ds(h * D, D)], st_att.at[h]) for h in range(G)
    ]
    for copy in att_out:
        copy.start()
    acc[...] = jnp.zeros_like(acc)

    def back(i):
        key, value = kv[i, 0], kv[i, 1]
        dk = jnp.zeros((D, 2 * T), F32)
        dv = jnp.zeros((D, 2 * T), F32)
        for t in range(ROWS // CHUNK):
            rows = pl.ds(t * CHUNK, CHUNK)
            p = pbuf[i, rows]
            delta = lrow[rows]
            ds = dot(gs[rows], value, NT) - jnp.concatenate([delta, delta], axis=1)
            ds = (p.astype(F32) * ds).astype(BF16)
            acc[rows] += dot(ds, key, NN)
            dk += dot(qt[:, rows], ds, NN)
            dv += dot(gt[:, rows], p, NN)
        part[i, 0] = dk[:, :T]
        part[i, 1] = dv[:, :T]
        s1[i, 0] = dk[:, T:].astype(BF16)
        s1[i, 1] = dv[:, T:].astype(BF16)

    def swap(i):
        return send(s1.at[i], r1.at[i], g1_s.at[i], g1_r.at[i], mate)

    def home(d):
        return send(s2.at[2 * d], r2.at[d], g2_s.at[2 * d], g2_r.at[d], c - 4 * d)

    def to_relay(i):
        d = (i + 1) // 2 - z
        return send(s2.at[i], r3.at[d], g2_s.at[i], g3_r.at[d], c - 4 * d)

    def back_across():
        return send(s3, r4, g4_s, g4_r, across)

    def child(d):
        return (c + 4 * d < n_ctx) & (2 * d - 1 + 2 * z < PAIRS)

    def order(n):
        return jnp.where(n < 4, 2 * n + 1, 16 - 2 * n)

    def pass_on(i):
        @pl.when(c >= 2 * i)
        def _():
            swap(i).wait_recv()
            total = part[i] + r1[i].astype(F32)
            part[i] = total
            s2[i] = total.astype(BF16)

            @pl.when(lax.rem(i, 2) == 0)
            def _():
                home(i // 2).start()

            @pl.when((lax.rem(i, 2) == 1) & ((z == 0) | (i > 1)))
            def _():
                to_relay(i).start()

    def backward(n, _):
        i = order(n)
        back(i)

        @pl.when(c >= 2 * i)
        def _():
            swap(i).start()

        @pl.when(n > 0)
        def _():
            pass_on(order(n - 1))

        @pl.when(n == 6)
        def _():
            for d in range(1, 5):

                @pl.when(child(d))
                def _():
                    send(s2.at[0], r3.at[d], g2_s.at[0], g3_r.at[d], mate).wait_recv()

            total = r3[1].astype(F32) + r3[2].astype(F32) + r3[3].astype(F32) + r3[4].astype(F32)
            total = total + part[1] * z.astype(F32)
            s3[...] = total.astype(BF16)
            back_across().start()

        return 0

    lax.fori_loop(0, PAIRS, backward, 0)

    for h in range(G):
        rows = pl.ds(h * T, T)
        dqo[rows] = (acc[rows] * SCALE).astype(BF16)
    dq_out = [
        pltpu.make_async_copy(dqo.at[pl.ds(h * T, T)], dq_hbm.at[:, pl.ds(h * D, D)], st_dq.at[h]) for h in range(G)
    ]
    for copy in dq_out:
        copy.start()

    swap(0).wait_recv()
    total = part[0] + r1[0].astype(F32)
    for d in range(1, 5):

        @pl.when(c + 4 * d < n_ctx)
        def _():
            send(s2.at[0], r2.at[d], g2_s.at[0], g2_r.at[d], mate).wait_recv()

    for d in range(1, 5):
        total = total + r2[d].astype(F32)
    back_across().wait_recv()
    total = total + r4[...].astype(F32)
    fin[0] = (total[0].T * SCALE).astype(BF16)
    fin[1] = total[1].T.astype(BF16)
    kv_out = [pltpu.make_async_copy(fin.at[j], ref, st_kv.at[j]) for j, ref in enumerate((dk_hbm, dv_hbm))]
    for copy in kv_out:
        copy.start()

    for kind in range(2):
        z_send(kind).wait_send()
        for d in range(1, 5):

            @pl.when(c + 4 * d < n_ctx)
            def _():
                own_send(d, kind).wait_send()

            @pl.when(relays(d))
            def _():
                relay_send(d, kind).wait_send()

        for i in range(PAIRS):

            @pl.when(c >= 2 * i)
            def _():
                forward(i, kind).wait_send()


    for i in range(PAIRS):

        @pl.when(c >= 2 * i)
        def _():
            swap(i).wait_send()
            if i > 0 and i % 2 == 0:
                home(i // 2).wait_send()
            if i > 1 and i % 2 == 1:
                to_relay(i).wait_send()

    @pl.when((z == 0) & (c >= 2))
    def _():
        to_relay(1).wait_send()

    back_across().wait_send()
    for copy in att_out + dq_out + kv_out:
        copy.wait()


def solution(mesh):
    n_ctx = mesh.shape["ctx"]

    def on_device(queries, key_rows, value_rows, out_grad, doc_lengths):
        anywhere = pl.BlockSpec(memory_space=pl.ANY)
        dma = pltpu.SemaphoreType.DMA
        vmem = pltpu.VMEM
        return pl.pallas_call(
            functools.partial(kernel, n_ctx),
            out_shape=(
                jax.ShapeDtypeStruct(queries.shape, BF16),
                jax.ShapeDtypeStruct(queries.shape, BF16),
                jax.ShapeDtypeStruct(key_rows.shape, BF16),
                jax.ShapeDtypeStruct(value_rows.shape, BF16),
            ),
            in_specs=[anywhere] * 4 + [pl.BlockSpec(memory_space=pltpu.SMEM)],
            out_specs=(anywhere,) * 4,
            scratch_shapes=[
                vmem((PAIRS + 1, 2, 2 * T, D), BF16),
                vmem((ROWS, D), BF16),
                vmem((ROWS, D), BF16),
                vmem((D, ROWS), BF16),
                vmem((D, ROWS), BF16),
                vmem((PAIRS, ROWS, 2 * T), F32),
                vmem((PAIRS, ROWS, 2 * T), BF16),
                vmem((PAIRS, T, 2 * T), F32),
                vmem((ROWS, T), F32),
                vmem((ROWS, T), F32),
                vmem((ROWS, D), F32),
                vmem((ROWS, D), BF16),
                vmem((ROWS, D), BF16),
                vmem((PAIRS, 2, D, T), F32),
                vmem((PAIRS, 2, D, T), BF16),
                vmem((PAIRS, 2, D, T), BF16),
                vmem((PAIRS, 2, D, T), BF16),
                vmem((5, 2, D, T), BF16),
                vmem((5, 2, D, T), BF16),
                vmem((2, D, T), BF16),
                vmem((2, D, T), BF16),
                vmem((2, T, D), BF16),
                dma((G,)), dma((G,)), dma((2,)), dma((G,)), dma((G,)), dma((2,)),
                dma((2,)), dma((5, 2)), dma((5, 2)), dma((PAIRS, 2)), dma((PAIRS + 1, 2)), dma((PAIRS, 2)),
                dma((PAIRS,)), dma((PAIRS,)), dma((PAIRS,)), dma((5,)), dma((5,)), dma, dma,
            ],
            compiler_params=pltpu.CompilerParams(
                collective_id=0, has_side_effects=True, vmem_limit_bytes=60 * 1024 * 1024
            ),
        )(queries, key_rows, value_rows, out_grad, doc_lengths)

    split = P("ctx", "head")
    return jax.shard_map(
        on_device, mesh=mesh, in_specs=(split, split, split, split, P()), out_specs=(split,) * 4, check_vma=False
    )
```

time: 633 us -> 65.4 us (0.10)
  waiting for transfers between devices: 300 us -> 0 us
  starting transfers between devices: 266 us -> 0 us
  Pallas kernels: 0 us -> 60.5 us
  matrix products: 25.2 us -> 0 us
  other arithmetic: 21.7 us -> 0 us
  local copies, waits for them, and re-layouts: 11.1 us -> 3.86 us
    ppermute x32 -> x0, waiting for transfers between devices: 300 us -> none  [from_behind(): lax.ppermute(value, axis, [(source, source + steps) for source in range(l...]
    ppermute x32 -> x0, starting transfers between devices: 266 us -> none  [from_behind(): lax.ppermute(value, axis, [(source, source + steps) for source in range(l...]
    pallas_call x0 -> x1, Pallas kernels: none -> 60.5 us  [on_device(): pl.pallas_call(functools.partial(kernel, n_ctx), out_shape=(jax.ShapeDtyp...]
    dot_general x12 -> x0, matrix products: 25.2 us -> none  [the longest x2 8.83 us: row_block(): lax.dot_general(rounded, grad_block, (((0,), (0,)), ((), ())), preferred_...]
    add x20 -> x0, other arithmetic: 14.8 us -> none  [the longest x16 14.7 us: giveback(): incoming + lax.dynamic_index_in_dim(grad_parts, reach_back - 1 - loop_ind...]
  transfers between devices with their start and end apart: 32 -> 0, of which waited for: 32 -> 0; matrix products, arithmetic and copies ran while one was open for 0% -> 0% of each run, Pallas kernels for 0% -> 0%
where the time goes in v1:
time: 65.4 us; the launch traced here: 65 us
  Pallas kernels  60.5 us (93%)
  local copies, waits for them, and re-layouts  3.86 us (6%)
    pallas_call x1, Pallas kernels, on_device(): pl.pallas_call(functools.partial(kernel, n_ctx), out_shape=(jax.ShapeDtyp...  60.5 us
    unnamed x10, local copies, waits for them, and re-layouts  3.86 us

profile of v1, /device:TPU:6, one launch (start us, length us, event | category | flops | bytes accessed | tf_op | source)
XLA Modules:
  0.0 65.0 jit_solution(6768181274918617446)
XLA Ops:
  0.6 60.5 %shard_map.84 = (bf16[128,1024]{1,0:T(8,128)(2,1)}, bf16[128,1024]{1,0:T(8,128)(2,1)}, bf16[128,128]{1,0:T(8,128)(2,1)}, bf16[128,128]{1,0:T(8,128)(2,1)}) custom-call(bf16[128,1024]{1,0:T(8,128)(2,1)} %q_hbm.1, bf16[128,128]{1,0:T(8,128)(2,1)} %k_hbm.1, bf16[128,128]{1,0:T(8,128)(2,1)} %v_hbm.1, bf16[128,1024]{1,0:T(8,128)(2,1)} %g_hbm.1, s32[16]{0:T(128)} %lengths.1), custom_call_target="tpu_custom_call" | custom-call | tf_op jit(solution)/shard_map/pallas_call | solution.py:412
  61.1 0.0 copy-start
  61.1 1.7 %copy.13 = bf16[128,1024]{1,0:T(8,128)(2,1)} copy(bf16[128,1024]{1,0:T(8,128)(2,1)} %get-tuple-element.8) | data formatting | bytes 524288
  62.8 0.0 copy-done
  62.8 0.0 copy-start.2
  62.8 0.7 %copy.14 = bf16[128,1024]{1,0:T(8,128)(2,1)} copy(bf16[128,1024]{1,0:T(8,128)(2,1)S(1)} %copy-done) | data formatting | bytes 524288
  63.5 0.1 copy-done.2
  63.6 0.0 copy-start.1
  63.6 0.6 copy.15
  64.2 0.2 copy-done.1
  64.4 0.6 copy.16
Async XLA Ops:
  61.1 1.7 %copy-start = (bf16[128,1024]{1,0:T(8,128)(2,1)S(1)}, bf16[128,1024]{1,0:T(8,128)(2,1)}, u32[]{:S(2)}) copy-start(bf16[128,1024]{1,0:T(8,128)(2,1)} %get-tuple-element.9) | copy-start | bytes 786436
  62.8 0.8 %copy-start.2 = (bf16[128,128]{1,0:T(8,128)(2,1)S(1)}, bf16[128,128]{1,0:T(8,128)(2,1)}, u32[]{:S(2)}) copy-start(bf16[128,128]{1,0:T(8,128)(2,1)} %get-tuple-element.10) | copy-start | bytes 98308
  63.6 0.8 %copy-start.1 = (bf16[128,128]{1,0:T(8,128)(2,1)S(1)}, bf16[128,128]{1,0:T(8,128)(2,1)}, u32[]{:S(2)}) copy-start(bf16[128,128]{1,0:T(8,128)(2,1)} %get-tuple-element.11) | copy-start | bytes 98308

commit v2 on v1

v2 whole, which is shorter than its diff:
```python
import functools
import math

import jax
import jax.numpy as jnp
from jax import lax
from jax.experimental import pallas as pl
from jax.experimental.pallas import tpu as pltpu
from jax.sharding import PartitionSpec as P

MESH = pl.DeviceIdType.MESH
T = 128
D = 128
G = 8
ROWS = T * G
PAIRS = 9
CHUNK = 256
NEG = -1e30
SCALE = D**-0.5
LOG2 = SCALE * math.log2(math.e)
NT = (((1,), (1,)), ((), ()))
NN = (((1,), (0,)), ((), ()))
F32, BF16 = jnp.float32, jnp.bfloat16


def dot(a, b, dims):
    return lax.dot_general(a, b, dims, preferred_element_type=F32)


def kernel(
    n_ctx,
    q_hbm, k_hbm, v_hbm, g_hbm, lengths,
    att_hbm, dq_hbm, dk_hbm, dv_hbm,
    kv, qs, gs, g2, qt, gt, sbuf, pbuf, dsb, bias, m1, m2, l1, l2, acc, att, dqo,
    part, s1, r1, s2, r2, r3, s3, r4, fin, transit,
    ld_q, ld_g, ld_kv, st_att, st_dq, st_kv,
    z_s, t_s, t_r, own_s, rel_s, fwd_s, kr, fr, g1_s, g1_r, g2_s, g2_r, g3_r, g4_s, g4_r,
):
    c = lax.axis_index("ctx")
    z = lax.rem(c // 2, 2)
    core = lax.rem(c, 2)
    mate = c + 1 - 2 * core
    across = c + 2 - 4 * z

    def along_z(step):
        at = lax.rem(z * 8 + lax.axis_index("head") + step, 16)
        return {"ctx": c - 2 * z + 2 * (at // 8), "head": lax.rem(at, 8)}, at // 8

    ahead, z_ahead = along_z(4 + 8 * core)
    behind, _ = along_z(12 - 8 * core)
    low, high = pl.ds(0, T), pl.ds(T, T)

    def send(src, dst, ss, rs, dev):
        return pltpu.make_async_remote_copy(
            src_ref=src, dst_ref=dst, send_sem=ss, recv_sem=rs, device_id=dev if isinstance(dev, dict) else {"ctx": dev}, device_id_type=MESH
        )

    own_in = [
        pltpu.make_async_copy(src, kv.at[0, kind, low], ld_kv.at[kind]) for kind, src in enumerate((k_hbm, v_hbm))
    ]
    q_in = [
        pltpu.make_async_copy(q_hbm.at[:, pl.ds(h * D, D)], qs.at[pl.ds(h * T, T)], ld_q.at[h]) for h in range(G)
    ]
    g_in = [
        pltpu.make_async_copy(g_hbm.at[:, pl.ds(h * D, D)], gs.at[pl.ds(h * T, T)], ld_g.at[h]) for h in range(G)
    ]
    for copy in own_in:
        copy.start()

    barrier = pltpu.get_barrier_semaphore()
    for dev in ({"ctx": mate}, ahead, behind):
        pl.semaphore_signal(barrier, inc=1, device_id=dev, device_id_type=MESH)
    count = 3
    for d in range(1, 5):
        up, down = c + 4 * d < n_ctx, c - 4 * d >= 0
        count = count + up.astype(jnp.int32) + down.astype(jnp.int32)

        @pl.when(up)
        def _():
            pl.semaphore_signal(barrier, inc=1, device_id={"ctx": c + 4 * d}, device_id_type=MESH)

        @pl.when(down)
        def _():
            pl.semaphore_signal(barrier, inc=1, device_id={"ctx": c - 4 * d}, device_id_type=MESH)

    for copy in q_in + g_in:
        copy.start()

    for i in range(1, PAIRS):

        @pl.when(c < 2 * i)
        def _():
            kv[i] = jnp.zeros((2, 2 * T, D), BF16)

    for d in range(1, 5):

        @pl.when(c + 4 * d >= n_ctx)
        def _():
            r2[d] = jnp.zeros((2, D, T), BF16)

        @pl.when((c + 4 * d >= n_ctx) | (2 * d - 1 + 2 * z >= PAIRS))
        def _():
            r3[d] = jnp.zeros((2, D, T), BF16)

    for copy in own_in:
        copy.wait()
    pl.semaphore_wait(barrier, count)

    land = 9 - 8 * z_ahead
    here = 9 - 8 * z

    def z_send(kind):
        return send(kv.at[0, kind, low], transit.at[kind], z_s.at[kind], t_r.at[kind], ahead)

    def z_pass(kind):
        return send(transit.at[kind], kv.at[land, kind, low], t_s.at[kind], kr.at[land, kind], ahead)

    def pass_along(kind):
        z_send(kind).wait_recv()
        z_pass(kind).start()

    def own_send(d, kind):
        return send(
            kv.at[0, kind, low], kv.at[2 * d, kind, low], own_s.at[d, kind], kr.at[2 * d, kind], c + 4 * d
        )

    def relay_send(d, kind):
        to = 2 * d - 1 + 2 * z
        return send(kv.at[here, kind, low], kv.at[to, kind, low], rel_s.at[d, kind], kr.at[to, kind], c + 4 * d)

    def forward(i, kind):
        return send(kv.at[i, kind, low], kv.at[i, kind, high], fwd_s.at[i, kind], fr.at[i, kind], mate)

    def arrived(i, kind):
        return send(kv.at[i, kind, low], kv.at[i, kind, low], z_s.at[kind], kr.at[i, kind], mate)

    relays = lambda d: (c + 4 * d < n_ctx) & (2 * d - 1 + 2 * z < PAIRS)

    def start_sends(kind):
        z_send(kind).start()
        for d in (2, 1, 3, 4):

            @pl.when(c + 4 * d < n_ctx)
            def _():
                own_send(d, kind).start()

        forward(0, kind).start()

    start_sends(0)

    row = c * T + lax.broadcasted_iota(jnp.int32, (T, 2 * T), 0)
    lane = lax.broadcasted_iota(jnp.int32, (T, 2 * T), 1)
    doc = jnp.zeros((T, 2 * T), jnp.int32)
    start = jnp.int32(0)
    for j in range(lengths.shape[0]):
        doc = jnp.where(row >= start, start, doc)
        start = start + lengths[j]
    first = lane + jnp.where(lane < T, c * T, mate * T - T)

    def mask(i, _):
        key = first - i * (2 * T)
        bias[i] = jnp.where((key >= doc) & (key <= row), 0.0, NEG)
        return 0

    lax.fori_loop(0, PAIRS, mask, 0)
    for copy in q_in:
        copy.wait()
    m1[...] = jnp.full_like(m1, NEG)
    m2[...] = jnp.full_like(m2, NEG)
    for ref in (l1, l2, acc):
        ref[...] = jnp.zeros_like(ref)

    def scores(i, most):
        key = kv[i, 0]
        b = bias[i]
        b = jnp.concatenate([b, b], axis=0)
        for t in range(ROWS // CHUNK):
            rows = pl.ds(t * CHUNK, CHUNK)
            s = dot(qs[rows], key, NT) + b
            sbuf[i, rows] = s
            most[rows] = jnp.maximum(most[rows], jnp.maximum(s[:, :T], s[:, T:]))

    def wide(x):
        return jnp.concatenate([x, x], axis=1)

    def weigh(i, most, total):
        for t in range(ROWS // CHUNK):
            rows = pl.ds(t * CHUNK, CHUNK)
            p = jnp.exp2((sbuf[i, rows] - wide(most[rows])) * LOG2)
            total[rows] += p[:, :T] + p[:, T:]
            pbuf[i, rows] = p.astype(BF16)

    def spread(x):
        return jnp.broadcast_to(x, (x.shape[0], T))

    def take(i, kind):
        @pl.when(c >= 2 * i)
        def _():
            arrived(i, kind).wait_recv()
            forward(i, kind).start()

    def await_mate(i, kind):
        @pl.when(c >= 2 * i)
        def _():
            forward(i, kind).wait_recv()

    def near_scores(n, _):
        i = 2 * n

        @pl.when(n == 1)
        def _():
            start_sends(1)
            pass_along(0)

        @pl.when(n < 4)
        def _():
            take(i + 2, 0)

        await_mate(i, 0)
        scores(i, m1)
        return 0

    lax.fori_loop(0, 5, near_scores, 0)
    for h in range(G):
        rows = pl.ds(h * T, T)
        m1[rows] = spread(jnp.max(m1[rows], axis=1, keepdims=True))
        qt[:, rows] = qs[rows].T

    def near_weigh(n, _):
        i = 2 * n

        @pl.when(n < 4)
        def _():
            take(i + 2, 1)

        @pl.when(n == 2)
        def _():
            pass_along(1)

        await_mate(i, 1)
        weigh(i, m1, l1)
        for t in range(ROWS // CHUNK):
            rows = pl.ds(t * CHUNK, CHUNK)
            acc[rows] += dot(pbuf[i, rows], kv[i, 1], NN)
        return 0

    lax.fori_loop(0, 5, near_weigh, 0)
    for h in range(G):
        rows = pl.ds(h * T, T)
        l1[rows] = spread(jnp.sum(l1[rows], axis=1, keepdims=True))
    for copy in g_in:
        copy.wait()

    for kind in range(2):
        arrived(here, kind).wait_recv()
        for d in range(1, 5):

            @pl.when(relays(d))
            def _():
                relay_send(d, kind).start()

        @pl.when(z == 1)
        def _():
            forward(1, kind).start()

    @pl.when(z == 0)
    def _():
        take(1, 0)

    take(3, 0)

    def far_scores(n, _):
        i = 2 * n + 1

        @pl.when(n < 2)
        def _():
            take(i + 4, 0)

        await_mate(i, 0)
        scores(i, m2)
        return 0

    lax.fori_loop(0, 4, far_scores, 0)

    @pl.when(z == 0)
    def _():
        take(1, 1)

    for i in (3, 5, 7):
        take(i, 1)

    for h in range(G):
        rows = pl.ds(h * T, T)
        old = m1[rows]
        most = jnp.maximum(old, spread(jnp.max(m2[rows], axis=1, keepdims=True)))
        m2[rows] = most
        m1[rows] = jnp.exp2((old - most) * LOG2)

    def far_weigh(n, _):
        weigh(2 * n + 1, m2, l2)
        return 0

    lax.fori_loop(0, 4, far_weigh, 0)
    for h in range(G):
        rows = pl.ds(h * T, T)
        inverse = 1.0 / (m1[rows] * l1[rows] + spread(jnp.sum(l2[rows], axis=1, keepdims=True)))
        l2[rows] = inverse
        grad = (gs[rows].astype(F32) * inverse).astype(BF16)
        g2[rows] = grad
        gt[:, rows] = grad.T

    def swap(i, kind):
        return send(s1.at[i, kind], r1.at[i, kind], g1_s.at[i, kind], g1_r.at[i, kind], mate)

    def home(d, kind):
        return send(s2.at[2 * d, kind], r2.at[d, kind], g2_s.at[2 * d, kind], g2_r.at[d, kind], c - 4 * d)

    def to_relay(i, kind):
        d = (i + 1) // 2 - z
        return send(s2.at[i, kind], r3.at[d, kind], g2_s.at[i, kind], g3_r.at[d, kind], c - 4 * d)

    def back_across(kind):
        return send(s3.at[kind], r4.at[kind], g4_s.at[kind], g4_r.at[kind], across)

    def child(d):
        return (c + 4 * d < n_ctx) & (2 * d - 1 + 2 * z < PAIRS)

    def give(i, kind, value):
        part[i, kind] = value[:, :T]
        s1[i, kind] = value[:, T:].astype(BF16)

        @pl.when(c >= 2 * i)
        def _():
            swap(i, kind).start()

    def pass_far(i, kind):
        @pl.when(c >= 2 * i)
        def _():
            swap(i, kind).wait_recv()
            total = part[i, kind] + r1[i, kind].astype(F32)
            part[i, kind] = total
            s2[i, kind] = total.astype(BF16)

            @pl.when((z == 0) | (i > 1))
            def _():
                to_relay(i, kind).start()

    def pass_near(i):
        @pl.when(c >= 2 * i)
        def _():
            for kind in range(2):
                swap(i, kind).wait_recv()
                s2[i, kind] = (part[i, kind] + r1[i, kind].astype(F32)).astype(BF16)
                home(i // 2, kind).start()

    def relay_back(kind):
        for d in range(1, 5):

            @pl.when(child(d))
            def _():
                send(s2.at[0, kind], r3.at[d, kind], g2_s.at[0, kind], g3_r.at[d, kind], mate).wait_recv()

        total = r3[1, kind].astype(F32) + r3[2, kind].astype(F32) + r3[3, kind].astype(F32) + r3[4, kind].astype(F32)
        s3[kind] = (total + part[1, kind] * z.astype(F32)).astype(BF16)
        back_across(kind).start()

    def far_values(n, _):
        i = 2 * n + 1
        give(i, 1, dot(gt[...], pbuf[i], NN))
        return 0

    lax.fori_loop(0, 4, far_values, 0)

    for n in range(4):
        await_mate(2 * n + 1, 1)

    def attend(t, _):
        rows = pl.ds(pl.multiple_of(t * CHUNK, CHUNK), CHUNK)
        total = acc[rows] * m1[rows]
        for i in (1, 3, 5, 7):
            total = total + dot(pbuf[i, rows], kv[i, 1], NN)
        inverse = l2[rows]
        out = (total * inverse).astype(BF16)
        att[rows] = out
        delta = jnp.sum(g2[rows].astype(F32) * out.astype(F32), axis=1, keepdims=True)
        l1[rows] = spread(delta)
        return 0

    lax.fori_loop(0, ROWS // CHUNK, attend, 0)

    def pass_values(n, _):
        pass_far(2 * n + 1, 1)
        return 0

    lax.fori_loop(0, 4, pass_values, 0)

    def score_grads(i, grads, deltas):
        value = kv[i, 1]
        for t in range(ROWS // CHUNK):
            rows = pl.ds(t * CHUNK, CHUNK)
            ds = dot(grads[rows], value, NT) - wide(deltas[rows])
            dsb[i, rows] = (pbuf[i, rows].astype(F32) * ds).astype(BF16)
        give(i, 0, dot(qt[...], dsb[i], NN))

    def far_keys(n, _):
        score_grads(2 * n + 1, g2, l1)

        @pl.when(n > 1)
        def _():
            pass_far(2 * n - 3, 0)

        return 0

    lax.fori_loop(0, 4, far_keys, 0)
    att_out = [
        pltpu.make_async_copy(att.at[pl.ds(h * T, T)], att_hbm.at[:, pl.ds(h * D, D)], st_att.at[h]) for h in range(G)
    ]
    for copy in att_out:
        copy.start()
    for h in range(G):
        rows = pl.ds(h * T, T)
        grad = (gs[rows].astype(F32) * (l2[rows] * m1[rows])).astype(BF16)
        gs[rows] = grad
        gt[:, rows] = grad.T
        l1[rows] = spread(jnp.sum(grad.astype(F32) * att[rows].astype(F32), axis=1, keepdims=True))
    pass_far(5, 0)
    pass_far(7, 0)

    def near(n, _):
        i = 8 - 2 * n
        give(i, 1, dot(gt[...], pbuf[i], NN))
        score_grads(i, gs, l1)

        @pl.when(n == 1)
        def _():
            relay_back(1)

        @pl.when(n > 1)
        def _():
            pass_near(i + 4)

        @pl.when(n == 2)
        def _():
            relay_back(0)

        return 0

    lax.fori_loop(0, 5, near, 0)
    pass_near(2)

    def query_grads(t, _):
        rows = pl.ds(pl.multiple_of(t * CHUNK, CHUNK), CHUNK)
        total = dot(dsb[0, rows], kv[0, 0], NN)
        for i in range(1, PAIRS):
            total = total + dot(dsb[i, rows], kv[i, 0], NN)
        dqo[rows] = (total * SCALE).astype(BF16)
        return 0

    lax.fori_loop(0, ROWS // CHUNK, query_grads, 0)
    dq_out = [
        pltpu.make_async_copy(dqo.at[pl.ds(h * T, T)], dq_hbm.at[:, pl.ds(h * D, D)], st_dq.at[h]) for h in range(G)
    ]
    for copy in dq_out:
        copy.start()

    for kind in range(2):
        swap(0, kind).wait_recv()
        for d in range(1, 5):

            @pl.when(c + 4 * d < n_ctx)
            def _():
                send(s2.at[0, kind], r2.at[d, kind], g2_s.at[0, kind], g2_r.at[d, kind], mate).wait_recv()

        total = part[0, kind] + r1[0, kind].astype(F32)
        for d in range(1, 5):
            total = total + r2[d, kind].astype(F32)
        part[0, kind] = total
    for kind in range(2):
        z_send(kind).wait_send()
        z_pass(kind).wait_send()
        for d in range(1, 5):

            @pl.when(c + 4 * d < n_ctx)
            def _():
                own_send(d, kind).wait_send()

            @pl.when(relays(d))
            def _():
                relay_send(d, kind).wait_send()

        for i in range(PAIRS):

            @pl.when(c >= 2 * i)
            def _():
                forward(i, kind).wait_send()


    for i in range(PAIRS):

        @pl.when(c >= 2 * i)
        def _():
            for kind in range(2):
                swap(i, kind).wait_send()
                if i > 0 and i % 2 == 0:
                    home(i // 2, kind).wait_send()
                if i > 1 and i % 2 == 1:
                    to_relay(i, kind).wait_send()

    @pl.when((z == 0) & (c >= 2))
    def _():
        for kind in range(2):
            to_relay(1, kind).wait_send()

    for copy in att_out + dq_out:
        copy.wait()
    kv_out = [pltpu.make_async_copy(fin.at[j], ref, st_kv.at[j]) for j, ref in enumerate((dk_hbm, dv_hbm))]
    for kind in (1, 0):
        back_across(kind).wait_recv()
        total = part[0, kind] + r4[kind].astype(F32)
        fin[kind] = (total.T * (1.0 if kind else SCALE)).astype(BF16)
        kv_out[kind].start()

    for kind in range(2):
        back_across(kind).wait_send()
    for copy in kv_out:
        copy.wait()


def hand_over(*refs):
    sources, outs, held, sem_in, sem_out = refs[:4], refs[4:8], refs[8:12], refs[12], refs[13]
    into = [pltpu.make_async_copy(a, b, sem_in.at[j]) for j, (a, b) in enumerate(zip(sources, held))]
    out = [pltpu.make_async_copy(a, b, sem_out.at[j]) for j, (a, b) in enumerate(zip(held, outs))]
    for copy in into:
        copy.start()
    for first, second in zip(into, out):
        first.wait()
        second.start()
    for copy in out:
        copy.wait()


def solution(mesh):
    n_ctx = mesh.shape["ctx"]

    def on_device(queries, key_rows, value_rows, out_grad, doc_lengths):
        anywhere = pl.BlockSpec(memory_space=pl.ANY)
        dma = pltpu.SemaphoreType.DMA
        vmem = pltpu.VMEM
        shapes = (
                jax.ShapeDtypeStruct(queries.shape, BF16),
                jax.ShapeDtypeStruct(queries.shape, BF16),
                jax.ShapeDtypeStruct(key_rows.shape, BF16),
                jax.ShapeDtypeStruct(value_rows.shape, BF16),
        )
        results = pl.pallas_call(
            functools.partial(kernel, n_ctx),
            out_shape=shapes,
            in_specs=[anywhere] * 4 + [pl.BlockSpec(memory_space=pltpu.SMEM)],
            out_specs=(anywhere,) * 4,
            scratch_shapes=[
                vmem((PAIRS + 1, 2, 2 * T, D), BF16),
                vmem((ROWS, D), BF16),
                vmem((ROWS, D), BF16),
                vmem((ROWS, D), BF16),
                vmem((D, ROWS), BF16),
                vmem((D, ROWS), BF16),
                vmem((PAIRS, ROWS, 2 * T), F32),
                vmem((PAIRS, ROWS, 2 * T), BF16),
                vmem((PAIRS, ROWS, 2 * T), BF16),
                vmem((PAIRS, T, 2 * T), F32),
                vmem((ROWS, T), F32),
                vmem((ROWS, T), F32),
                vmem((ROWS, T), F32),
                vmem((ROWS, T), F32),
                vmem((ROWS, D), F32),
                vmem((ROWS, D), BF16),
                vmem((ROWS, D), BF16),
                vmem((PAIRS, 2, D, T), F32),
                vmem((PAIRS, 2, D, T), BF16),
                vmem((PAIRS, 2, D, T), BF16),
                vmem((PAIRS, 2, D, T), BF16),
                vmem((5, 2, D, T), BF16),
                vmem((5, 2, D, T), BF16),
                vmem((2, D, T), BF16),
                vmem((2, D, T), BF16),
                vmem((2, T, D), BF16),
                vmem((2, T, D), BF16),
                dma((G,)), dma((G,)), dma((2,)), dma((G,)), dma((G,)), dma((2,)),
                dma((2,)), dma((2,)), dma((2,)), dma((5, 2)), dma((5, 2)), dma((PAIRS, 2)), dma((PAIRS + 1, 2)), dma((PAIRS, 2)),
                dma((PAIRS, 2)), dma((PAIRS, 2)), dma((PAIRS, 2)), dma((5, 2)), dma((5, 2)), dma((2,)), dma((2,)),
            ],
            compiler_params=pltpu.CompilerParams(
                collective_id=0, has_side_effects=True, vmem_limit_bytes=60 * 1024 * 1024
            ),
        )(queries, key_rows, value_rows, out_grad, doc_lengths)
        return pl.pallas_call(
            hand_over,
            out_shape=shapes,
            in_specs=[anywhere] * 4,
            out_specs=(anywhere,) * 4,
            scratch_shapes=[vmem(x.shape, x.dtype) for x in shapes] + [dma((4,)), dma((4,))],
            compiler_params=pltpu.CompilerParams(vmem_limit_bytes=62 * 1024 * 1024),
        )(*results)

    split = P("ctx", "head")
    return jax.shard_map(
        on_device, mesh=mesh, in_specs=(split, split, split, split, P()), out_specs=(split,) * 4, check_vma=False
    )
```

time: 65.4 us -> 57.2 us (0.87)
  Pallas kernels: 60.5 us -> 56.2 us
  local copies, waits for them, and re-layouts: 3.86 us -> 0 us
    pallas_call x1 -> x2, Pallas kernels: 60.5 us -> 56.2 us  [the longest x1 54.4 us: on_device(): pl.pallas_call(functools.partial(kernel, n_ctx), out_shape=shapes, in_spe...]
    unnamed x10 -> x0, local copies, waits for them, and re-layouts: 3.86 us -> none
where the time goes in v2:
time: 57.2 us; the launch traced here: 56.8 us
  Pallas kernels  56.2 us (98%)
  between operations  0.64 us (1%)
    pallas_call x1, Pallas kernels, on_device(): pl.pallas_call(functools.partial(kernel, n_ctx), out_shape=shapes, in_spe...  54.4 us
    pallas_call x1, Pallas kernels, on_device(): pl.pallas_call(hand_over, out_shape=shapes, in_specs=[anywhere] * 4, out_...  1.82 us

profile of v2, /device:TPU:6, one launch (start us, length us, event | category | flops | bytes accessed | tf_op | source)
XLA Modules:
  0.0 56.8 jit_solution(7736306733109056424)
XLA Ops:
  0.6 54.4 %shard_map.84 = (bf16[128,1024]{1,0:T(8,128)(2,1)}, bf16[128,1024]{1,0:T(8,128)(2,1)}, bf16[128,128]{1,0:T(8,128)(2,1)}, bf16[128,128]{1,0:T(8,128)(2,1)}) custom-call(bf16[128,1024]{1,0:T(8,128)(2,1)} %q_hbm.1, bf16[128,128]{1,0:T(8,128)(2,1)} %k_hbm.1, bf16[128,128]{1,0:T(8,128)(2,1)} %v_hbm.1, bf16[128,1024]{1,0:T(8,128)(2,1)} %g_hbm.1, s32[16]{0:T(128)} %lengths.1), custom_call_target="tpu_custom_call" | custom-call | tf_op jit(solution)/shard_map/pallas_call | solution.py:555
  55.0 1.8 %shard_map.85 = (bf16[128,1024]{1,0:T(8,128)(2,1)}, bf16[128,1024]{1,0:T(8,128)(2,1)}, bf16[128,128]{1,0:T(8,128)(2,1)}, bf16[128,128]{1,0:T(8,128)(2,1)}) custom-call(bf16[128,1024]{1,0:T(8,128)(2,1)} %get-tuple-element.8.refs_0_, bf16[128,1024]{1,0:T(8,128)(2,1)} %get-tuple-element.9.refs_1_, bf16[128,128]{1,0:T(8,128)(2,1)} %get-tuple-element.10.refs_2_, ...), custom_call_target="tpu_custom_call" | custom-call | tf_op jit(solution)/shard_map/pallas_call | solution.py:596

commit v3 on v2

--- a/solution.py
+++ b/solution.py
@@ -30,11 +30,11 @@
 def kernel(
     n_ctx,
     q_hbm, k_hbm, v_hbm, g_hbm, lengths,
-    att_hbm, dq_hbm, dk_hbm, dv_hbm,
+    att_hbm, dq_hbm, sum_hbm, r4,
     kv, qs, gs, g2, qt, gt, sbuf, pbuf, dsb, bias, m1, m2, l1, l2, acc, att, dqo,
-    part, s1, r1, s2, r2, r3, s3, r4, fin, transit,
+    part, s1, r1, s2, r2, r3, s3, transit,
     ld_q, ld_g, ld_kv, st_att, st_dq, st_kv,
-    z_s, t_s, t_r, own_s, rel_s, fwd_s, kr, fr, g1_s, g1_r, g2_s, g2_r, g3_r, g4_s, g4_r,
+    z_s, t_s, t_r, own_s, rel_s, fwd_s, kr, fr, g1_r, g2_r, g3_r, g4_r,
 ):
     c = lax.axis_index("ctx")
     z = lax.rem(c // 2, 2)
@@ -55,14 +55,17 @@
             src_ref=src, dst_ref=dst, send_sem=ss, recv_sem=rs, device_id=dev if isinstance(dev, dict) else {"ctx": dev}, device_id_type=MESH
         )
 
+    def whole(ref, sem):
+        return pltpu.make_async_copy(ref, ref, sem)
+
     own_in = [
         pltpu.make_async_copy(src, kv.at[0, kind, low], ld_kv.at[kind]) for kind, src in enumerate((k_hbm, v_hbm))
     ]
     q_in = [
-        pltpu.make_async_copy(q_hbm.at[:, pl.ds(h * D, D)], qs.at[pl.ds(h * T, T)], ld_q.at[h]) for h in range(G)
+        pltpu.make_async_copy(q_hbm.at[:, pl.ds(h * D, D)], qs.at[pl.ds(h * T, T)], ld_q) for h in range(G)
     ]
     g_in = [
-        pltpu.make_async_copy(g_hbm.at[:, pl.ds(h * D, D)], gs.at[pl.ds(h * T, T)], ld_g.at[h]) for h in range(G)
+        pltpu.make_async_copy(g_hbm.at[:, pl.ds(h * D, D)], gs.at[pl.ds(h * T, T)], ld_g) for h in range(G)
     ]
     for copy in own_in:
         copy.start()
@@ -113,26 +116,41 @@
         return send(kv.at[0, kind, low], transit.at[kind], z_s.at[kind], t_r.at[kind], ahead)
 
     def z_pass(kind):
-        return send(transit.at[kind], kv.at[land, kind, low], t_s.at[kind], kr.at[land, kind], ahead)
+        return send(transit.at[kind], kv.at[land, kind, low], t_s.at[kind], kr.at[far(land, kind)], ahead)
 
     def pass_along(kind):
         z_send(kind).wait_recv()
         z_pass(kind).start()
 
     def own_send(d, kind):
-        return send(
-            kv.at[0, kind, low], kv.at[2 * d, kind, low], own_s.at[d, kind], kr.at[2 * d, kind], c + 4 * d
-        )
+        at = 4 * kind + d - 1
+        return send(kv.at[0, kind, low], kv.at[2 * d, kind, low], own_s.at[at], kr.at[at], c + 4 * d)
+
+    def far(i, kind):
+        return 8 + 5 * kind + (i - 1) // 2
+
+    def far_swapped(i, kind):
+        return 5 + 4 * kind + (i - 1) // 2
 
     def relay_send(d, kind):
         to = 2 * d - 1 + 2 * z
-        return send(kv.at[here, kind, low], kv.at[to, kind, low], rel_s.at[d, kind], kr.at[to, kind], c + 4 * d)
-
-    def forward(i, kind):
-        return send(kv.at[i, kind, low], kv.at[i, kind, high], fwd_s.at[i, kind], fr.at[i, kind], mate)
-
-    def arrived(i, kind):
-        return send(kv.at[i, kind, low], kv.at[i, kind, low], z_s.at[kind], kr.at[i, kind], mate)
+        return send(
+            kv.at[here, kind, low], kv.at[to, kind, low], rel_s.at[4 * kind + d - 1], kr.at[far(to, kind)], c + 4 * d
+        )
+
+    def near_forward(i, kind):
+        at = 5 * kind + i // 2
+        return send(kv.at[i, kind, low], kv.at[i, kind, high], fwd_s.at[at], fr.at[at], mate)
+
+    def far_forward(i, kind):
+        at = far_swapped(i, kind) + 5
+        return send(kv.at[i, kind, low], kv.at[i, kind, high], fwd_s.at[at], fr.at[at], mate)
+
+    def near_arrived(i, kind):
+        return send(kv.at[i, kind, low], kv.at[i, kind, low], z_s.at[0], kr.at[4 * kind + i // 2 - 1], mate)
+
+    def far_arrived(i, kind):
+        return send(kv.at[i, kind, low], kv.at[i, kind, low], z_s.at[kind], kr.at[far(i, kind)], mate)
 
     relays = lambda d: (c + 4 * d < n_ctx) & (2 * d - 1 + 2 * z < PAIRS)
 
@@ -144,7 +162,7 @@
             def _():
                 own_send(d, kind).start()
 
-        forward(0, kind).start()
+        near_forward(0, kind).start()
 
     start_sends(0)
 
@@ -163,8 +181,7 @@
         return 0
 
     lax.fori_loop(0, PAIRS, mask, 0)
-    for copy in q_in:
-        copy.wait()
+    whole(qs, ld_q).wait()
     m1[...] = jnp.full_like(m1, NEG)
     m2[...] = jnp.full_like(m2, NEG)
     for ref in (l1, l2, acc):
@@ -193,16 +210,27 @@
     def spread(x):
         return jnp.broadcast_to(x, (x.shape[0], T))
 
-    def take(i, kind):
-        @pl.when(c >= 2 * i)
-        def _():
-            arrived(i, kind).wait_recv()
-            forward(i, kind).start()
-
-    def await_mate(i, kind):
-        @pl.when(c >= 2 * i)
-        def _():
-            forward(i, kind).wait_recv()
+    def take_near(i, kind):
+        @pl.when(c >= 2 * i)
+        def _():
+            near_arrived(i, kind).wait_recv()
+            near_forward(i, kind).start()
+
+    def await_near(i, kind):
+        @pl.when(c >= 2 * i)
+        def _():
+            near_forward(i, kind).wait_recv()
+
+    def take_far(i, kind):
+        @pl.when(c >= 2 * i)
+        def _():
+            far_arrived(i, kind).wait_recv()
+            far_forward(i, kind).start()
+
+    def await_far(i, kind):
+        @pl.when(c >= 2 * i)
+        def _():
+            far_forward(i, kind).wait_recv()
 
     def near_scores(n, _):
         i = 2 * n
@@ -214,9 +242,9 @@
 
         @pl.when(n < 4)
         def _():
-            take(i + 2, 0)
-
-        await_mate(i, 0)
+            take_near(i + 2, 0)
+
+        await_near(i, 0)
         scores(i, m1)
         return 0
 
@@ -231,13 +259,13 @@
 
         @pl.when(n < 4)
         def _():
-            take(i + 2, 1)
+            take_near(i + 2, 1)
 
         @pl.when(n == 2)
         def _():
             pass_along(1)
 
-        await_mate(i, 1)
+        await_near(i, 1)
         weigh(i, m1, l1)
         for t in range(ROWS // CHUNK):
             rows = pl.ds(t * CHUNK, CHUNK)
@@ -248,11 +276,10 @@
     for h in range(G):
         rows = pl.ds(h * T, T)
         l1[rows] = spread(jnp.sum(l1[rows], axis=1, keepdims=True))
-    for copy in g_in:
-        copy.wait()
+    whole(gs, ld_g).wait()
 
     for kind in range(2):
-        arrived(here, kind).wait_recv()
+        far_arrived(here, kind).wait_recv()
         for d in range(1, 5):
 
             @pl.when(relays(d))
@@ -261,22 +288,22 @@
 
         @pl.when(z == 1)
         def _():
-            forward(1, kind).start()
+            far_forward(1, kind).start()
 
     @pl.when(z == 0)
     def _():
-        take(1, 0)
-
-    take(3, 0)
+        take_far(1, 0)
+
+    take_far(3, 0)
 
     def far_scores(n, _):
         i = 2 * n + 1
 
         @pl.when(n < 2)
         def _():
-            take(i + 4, 0)
-
-        await_mate(i, 0)
+            take_far(i + 4, 0)
+
+        await_far(i, 0)
         scores(i, m2)
         return 0
 
@@ -284,10 +311,10 @@
 
     @pl.when(z == 0)
     def _():
-        take(1, 1)
+        take_far(1, 1)
 
     for i in (3, 5, 7):
-        take(i, 1)
+        take_far(i, 1)
 
     for h in range(G):
         rows = pl.ds(h * T, T)
@@ -309,34 +336,72 @@
         g2[rows] = grad
         gt[:, rows] = grad.T
 
-    def swap(i, kind):
-        return send(s1.at[i, kind], r1.at[i, kind], g1_s.at[i, kind], g1_r.at[i, kind], mate)
-
-    def home(d, kind):
-        return send(s2.at[2 * d, kind], r2.at[d, kind], g2_s.at[2 * d, kind], g2_r.at[d, kind], c - 4 * d)
+    def near_swap(i):
+        return send(s1.at[i], r1.at[i], fwd_s.at[i // 2], g1_r.at[i // 2], mate)
+
+    def far_swap(i, kind):
+        return send(s1.at[i, kind], r1.at[i, kind], fwd_s.at[far_swapped(i, 1 - kind) + 5], g1_r.at[far_swapped(i, kind)], mate)
+
+    def home(d):
+        return send(s2.at[2 * d], r2.at[d], own_s.at[d - 1], g2_r.at[d - 1], c - 4 * d)
 
     def to_relay(i, kind):
         d = (i + 1) // 2 - z
-        return send(s2.at[i, kind], r3.at[d, kind], g2_s.at[i, kind], g3_r.at[d, kind], c - 4 * d)
+        return send(
+            s2.at[i, kind], r3.at[d, kind], rel_s.at[4 - 4 * kind + (i - 1) // 2], g3_r.at[4 * kind + d - 1], c - 4 * d
+        )
 
     def back_across(kind):
-        return send(s3.at[kind], r4.at[kind], g4_s.at[kind], g4_r.at[kind], across)
+        return send(s3.at[kind], r4.at[kind], z_s.at[kind], g4_r.at[kind], across)
+
+    def gather_sent(kind):
+        z_send(kind).wait_send()
+        z_pass(kind).wait_send()
+        for d in range(1, 5):
+
+            @pl.when(relays(d))
+            def _():
+                relay_send(d, kind).wait_send()
+
+        for i in (1, 3, 5, 7):
+
+            @pl.when(c >= 2 * i)
+            def _():
+                far_forward(i, kind).wait_send()
+
+    def near_sent():
+        for d in range(1, 5):
+
+            @pl.when(c + 4 * d < n_ctx)
+            def _():
+                for kind in range(2):
+                    own_send(d, kind).wait_send()
+
+        for i in range(0, PAIRS, 2):
+
+            @pl.when(c >= 2 * i)
+            def _():
+                for kind in range(2):
+                    near_forward(i, kind).wait_send()
 
     def child(d):
         return (c + 4 * d < n_ctx) & (2 * d - 1 + 2 * z < PAIRS)
 
-    def give(i, kind, value):
+    def keep(i, kind, value):
         part[i, kind] = value[:, :T]
         s1[i, kind] = value[:, T:].astype(BF16)
 
-        @pl.when(c >= 2 * i)
-        def _():
-            swap(i, kind).start()
+    def give(i, kind, value):
+        keep(i, kind, value)
+
+        @pl.when(c >= 2 * i)
+        def _():
+            far_swap(i, kind).start()
 
     def pass_far(i, kind):
         @pl.when(c >= 2 * i)
         def _():
-            swap(i, kind).wait_recv()
+            far_swap(i, kind).wait_recv()
             total = part[i, kind] + r1[i, kind].astype(F32)
             part[i, kind] = total
             s2[i, kind] = total.astype(BF16)
@@ -348,31 +413,36 @@
     def pass_near(i):
         @pl.when(c >= 2 * i)
         def _():
-            for kind in range(2):
-                swap(i, kind).wait_recv()
-                s2[i, kind] = (part[i, kind] + r1[i, kind].astype(F32)).astype(BF16)
-                home(i // 2, kind).start()
+            near_swap(i).wait_recv()
+            s2[i] = (part[i] + r1[i].astype(F32)).astype(BF16)
+            home(i // 2).start()
 
     def relay_back(kind):
         for d in range(1, 5):
 
             @pl.when(child(d))
             def _():
-                send(s2.at[0, kind], r3.at[d, kind], g2_s.at[0, kind], g3_r.at[d, kind], mate).wait_recv()
+                send(s2.at[0, kind], r3.at[d, kind], z_s.at[kind], g3_r.at[4 * kind + d - 1], mate).wait_recv()
 
         total = r3[1, kind].astype(F32) + r3[2, kind].astype(F32) + r3[3, kind].astype(F32) + r3[4, kind].astype(F32)
         s3[kind] = (total + part[1, kind] * z.astype(F32)).astype(BF16)
         back_across(kind).start()
 
+    def far_pair(n):
+        up = jnp.where(n == 0, 3, jnp.where(n == 1, 5, jnp.where(n == 2, 1, 7)))
+        down = jnp.where(n == 0, 5, jnp.where(n == 1, 7, jnp.where(n == 2, 3, 1)))
+        return jnp.where(z == 0, up, down)
+
     def far_values(n, _):
-        i = 2 * n + 1
+        i = far_pair(n)
         give(i, 1, dot(gt[...], pbuf[i], NN))
         return 0
 
+    gather_sent(0)
     lax.fori_loop(0, 4, far_values, 0)
 
     for n in range(4):
-        await_mate(2 * n + 1, 1)
+        await_far(2 * n + 1, 1)
 
     def attend(t, _):
         rows = pl.ds(pl.multiple_of(t * CHUNK, CHUNK), CHUNK)
@@ -389,31 +459,33 @@
     lax.fori_loop(0, ROWS // CHUNK, attend, 0)
 
     def pass_values(n, _):
-        pass_far(2 * n + 1, 1)
+        pass_far(far_pair(n), 1)
         return 0
 
     lax.fori_loop(0, 4, pass_values, 0)
 
-    def score_grads(i, grads, deltas):
+    def score_grads(i, grads, deltas, after):
         value = kv[i, 1]
         for t in range(ROWS // CHUNK):
             rows = pl.ds(t * CHUNK, CHUNK)
             ds = dot(grads[rows], value, NT) - wide(deltas[rows])
             dsb[i, rows] = (pbuf[i, rows].astype(F32) * ds).astype(BF16)
-        give(i, 0, dot(qt[...], dsb[i], NN))
+        after(i, 0, dot(qt[...], dsb[i], NN))
 
     def far_keys(n, _):
-        score_grads(2 * n + 1, g2, l1)
+        score_grads(far_pair(n), g2, l1, give)
 
         @pl.when(n > 1)
         def _():
-            pass_far(2 * n - 3, 0)
-
-        return 0
-
+            pass_far(far_pair(n - 2), 0)
+
+        return 0
+
+    gather_sent(1)
     lax.fori_loop(0, 4, far_keys, 0)
+    near_sent()
     att_out = [
-        pltpu.make_async_copy(att.at[pl.ds(h * T, T)], att_hbm.at[:, pl.ds(h * D, D)], st_att.at[h]) for h in range(G)
+        pltpu.make_async_copy(att.at[pl.ds(h * T, T)], att_hbm.at[:, pl.ds(h * D, D)], st_att) for h in range(G)
     ]
     for copy in att_out:
         copy.start()
@@ -423,13 +495,17 @@
         gs[rows] = grad
         gt[:, rows] = grad.T
         l1[rows] = spread(jnp.sum(grad.astype(F32) * att[rows].astype(F32), axis=1, keepdims=True))
-    pass_far(5, 0)
-    pass_far(7, 0)
+    pass_far(far_pair(2), 0)
+    pass_far(far_pair(3), 0)
 
     def near(n, _):
         i = 8 - 2 * n
-        give(i, 1, dot(gt[...], pbuf[i], NN))
-        score_grads(i, gs, l1)
+        keep(i, 1, dot(gt[...], pbuf[i], NN))
+        score_grads(i, gs, l1, keep)
+
+        @pl.when(c >= 2 * i)
+        def _():
+            near_swap(i).start()
 
         @pl.when(n == 1)
         def _():
@@ -458,84 +534,71 @@
 
     lax.fori_loop(0, ROWS // CHUNK, query_grads, 0)
     dq_out = [
-        pltpu.make_async_copy(dqo.at[pl.ds(h * T, T)], dq_hbm.at[:, pl.ds(h * D, D)], st_dq.at[h]) for h in range(G)
+        pltpu.make_async_copy(dqo.at[pl.ds(h * T, T)], dq_hbm.at[:, pl.ds(h * D, D)], st_dq) for h in range(G)
     ]
     for copy in dq_out:
         copy.start()
 
+    near_swap(0).wait_recv()
+    for d in range(1, 5):
+
+        @pl.when(c + 4 * d < n_ctx)
+        def _():
+            send(s2.at[0], r2.at[d], z_s.at[0], g2_r.at[d - 1], mate).wait_recv()
+
     for kind in range(2):
-        swap(0, kind).wait_recv()
-        for d in range(1, 5):
-
-            @pl.when(c + 4 * d < n_ctx)
-            def _():
-                send(s2.at[0, kind], r2.at[d, kind], g2_s.at[0, kind], g2_r.at[d, kind], mate).wait_recv()
-
         total = part[0, kind] + r1[0, kind].astype(F32)
         for d in range(1, 5):
             total = total + r2[d, kind].astype(F32)
         part[0, kind] = total
-    for kind in range(2):
-        z_send(kind).wait_send()
-        z_pass(kind).wait_send()
-        for d in range(1, 5):
-
-            @pl.when(c + 4 * d < n_ctx)
-            def _():
-                own_send(d, kind).wait_send()
-
-            @pl.when(relays(d))
-            def _():
-                relay_send(d, kind).wait_send()
-
-        for i in range(PAIRS):
-
-            @pl.when(c >= 2 * i)
-            def _():
-                forward(i, kind).wait_send()
-
 
     for i in range(PAIRS):
 
         @pl.when(c >= 2 * i)
         def _():
-            for kind in range(2):
-                swap(i, kind).wait_send()
-                if i > 0 and i % 2 == 0:
-                    home(i // 2, kind).wait_send()
-                if i > 1 and i % 2 == 1:
-                    to_relay(i, kind).wait_send()
+            if i % 2 == 0:
+                near_swap(i).wait_send()
+                if i > 0:
+                    home(i // 2).wait_send()
+            else:
+                for kind in range(2):
+                    far_swap(i, kind).wait_send()
+                    if i > 1:
+                        to_relay(i, kind).wait_send()
 
     @pl.when((z == 0) & (c >= 2))
     def _():
         for kind in range(2):
             to_relay(1, kind).wait_send()
 
-    for copy in att_out + dq_out:
+    sums_out = pltpu.make_async_copy(part.at[0], sum_hbm, st_kv)
+    sums_out.start()
+    for copy in (whole(att, st_att), whole(dqo, st_dq), sums_out):
         copy.wait()
-    kv_out = [pltpu.make_async_copy(fin.at[j], ref, st_kv.at[j]) for j, ref in enumerate((dk_hbm, dv_hbm))]
+    for kind in range(2):
+        back_across(kind).wait_send()
     for kind in (1, 0):
         back_across(kind).wait_recv()
-        total = part[0, kind] + r4[kind].astype(F32)
-        fin[kind] = (total.T * (1.0 if kind else SCALE)).astype(BF16)
-        kv_out[kind].start()
-
-    for kind in range(2):
-        back_across(kind).wait_send()
-    for copy in kv_out:
-        copy.wait()
-
-
-def hand_over(*refs):
-    sources, outs, held, sem_in, sem_out = refs[:4], refs[4:8], refs[8:12], refs[12], refs[13]
-    into = [pltpu.make_async_copy(a, b, sem_in.at[j]) for j, (a, b) in enumerate(zip(sources, held))]
-    out = [pltpu.make_async_copy(a, b, sem_out.at[j]) for j, (a, b) in enumerate(zip(held, outs))]
+
+
+def finish(att_in, dq_in, sums_in, back_in, att_out, dq_out, dk_out, dv_out, att, dq, sums, back, out, sem_in, sem_out):
+    def copies(pairs, sems):
+        return [pltpu.make_async_copy(a, b, sems.at[j]) for j, (a, b) in enumerate(pairs)]
+
+    into = copies(((back_in, back), (sums_in, sums), (att_in, att), (dq_in, dq)), sem_in)
+    away = copies(((out.at[0], dk_out), (out.at[1], dv_out), (att, att_out), (dq, dq_out)), sem_out)
     for copy in into:
         copy.start()
-    for first, second in zip(into, out):
-        first.wait()
-        second.start()
-    for copy in out:
+    into[0].wait()
+    into[1].wait()
+    for kind, scale in enumerate((SCALE, 1.0)):
+        total = sums[kind] + back[kind].astype(F32)
+        out[kind] = (total.T * scale).astype(BF16)
+        away[kind].start()
+    for j in (2, 3):
+        into[j].wait()
+        away[j].start()
+    for copy in away:
         copy.wait()
 
 
@@ -546,15 +609,11 @@
         anywhere = pl.BlockSpec(memory_space=pl.ANY)
         dma = pltpu.SemaphoreType.DMA
         vmem = pltpu.VMEM
-        shapes = (
-                jax.ShapeDtypeStruct(queries.shape, BF16),
-                jax.ShapeDtypeStruct(queries.shape, BF16),
-                jax.ShapeDtypeStruct(key_rows.shape, BF16),
-                jax.ShapeDtypeStruct(value_rows.shape, BF16),
-        )
+        wide = jax.ShapeDtypeStruct(queries.shape, BF16)
+        narrow = jax.ShapeDtypeStruct(key_rows.shape, BF16)
         results = pl.pallas_call(
             functools.partial(kernel, n_ctx),
-            out_shape=shapes,
+            out_shape=(wide, wide, jax.ShapeDtypeStruct((2, D, T), F32), jax.ShapeDtypeStruct((2, D, T), BF16)),
             in_specs=[anywhere] * 4 + [pl.BlockSpec(memory_space=pltpu.SMEM)],
             out_specs=(anywhere,) * 4,
             scratch_shapes=[
@@ -582,23 +641,24 @@
                 vmem((5, 2, D, T), BF16),
                 vmem((5, 2, D, T), BF16),
                 vmem((2, D, T), BF16),
-                vmem((2, D, T), BF16),
                 vmem((2, T, D), BF16),
-                vmem((2, T, D), BF16),
-                dma((G,)), dma((G,)), dma((2,)), dma((G,)), dma((G,)), dma((2,)),
-                dma((2,)), dma((2,)), dma((2,)), dma((5, 2)), dma((5, 2)), dma((PAIRS, 2)), dma((PAIRS + 1, 2)), dma((PAIRS, 2)),
-                dma((PAIRS, 2)), dma((PAIRS, 2)), dma((PAIRS, 2)), dma((5, 2)), dma((5, 2)), dma((2,)), dma((2,)),
+                dma, dma, dma((2,)), dma, dma, dma,
+                dma((2,)), dma((2,)), dma((2,)), dma((8,)), dma((8,)), dma((18,)), dma((18,)), dma((18,)),
+                dma((13,)), dma((4,)), dma((8,)), dma((2,)),
             ],
             compiler_params=pltpu.CompilerParams(
                 collective_id=0, has_side_effects=True, vmem_limit_bytes=60 * 1024 * 1024
             ),
         )(queries, key_rows, value_rows, out_grad, doc_lengths)
         return pl.pallas_call(
-            hand_over,
-            out_shape=shapes,
+            finish,
+            out_shape=(wide, wide, narrow, narrow),
             in_specs=[anywhere] * 4,
             out_specs=(anywhere,) * 4,
-            scratch_shapes=[vmem(x.shape, x.dtype) for x in shapes] + [dma((4,)), dma((4,))],
+            scratch_shapes=[
+                vmem(wide.shape, BF16), vmem(wide.shape, BF16), vmem((2, D, T), F32), vmem((2, D, T), BF16),
+                vmem((2, T, D), BF16), dma((4,)), dma((4,)),
+            ],
             compiler_params=pltpu.CompilerParams(vmem_limit_bytes=62 * 1024 * 1024),
         )(*results)
 

time: 57.2 us -> 55.1 us (0.963)
  Pallas kernels: 56.2 us -> 54.2 us
    pallas_call x2, Pallas kernels: 56.2 us -> 54.2 us  [the longest x1 52.3 us: on_device(): pl.pallas_call(functools.partial(kernel, n_ctx), out_shape=(wide, wide, j...]
where the time goes in v3:
time: 55.1 us; the launch traced here: 54.9 us
  Pallas kernels  54.2 us (98%)
  between operations  0.64 us (1%)
    pallas_call x1, Pallas kernels, on_device(): pl.pallas_call(functools.partial(kernel, n_ctx), out_shape=(wide, wide, j...  52.3 us
    pallas_call x1, Pallas kernels, on_device(): pl.pallas_call(finish, out_shape=(wide, wide, narrow, narrow), in_specs=[...  1.93 us

profile of v3, /device:TPU:6, one launch (start us, length us, event | category | flops | bytes accessed | tf_op | source)
XLA Modules:
  0.0 54.9 jit_solution(10619391919997203516)
XLA Ops:
  0.6 52.3 %shard_map.84 = (bf16[128,1024]{1,0:T(8,128)(2,1)}, bf16[128,1024]{1,0:T(8,128)(2,1)}, f32[2,128,128]{2,1,0:T(8,128)}, bf16[2,128,128]{2,1,0:T(8,128)(2,1)}) custom-call(bf16[128,1024]{1,0:T(8,128)(2,1)} %q_hbm.1, bf16[128,128]{1,0:T(8,128)(2,1)} %k_hbm.1, bf16[128,128]{1,0:T(8,128)(2,1)} %v_hbm.1, bf16[128,1024]{1,0:T(8,128)(2,1)} %g_hbm.1, s32[16]{0:T(128)} %lengths.1), custom_call_target="tpu_custom_call" | custom-call | tf_op jit(solution)/shard_map/pallas_call | solution.py:614
  52.9 1.9 %shard_map.85 = (bf16[128,1024]{1,0:T(8,128)(2,1)}, bf16[128,1024]{1,0:T(8,128)(2,1)}, bf16[128,128]{1,0:T(8,128)(2,1)}, bf16[128,128]{1,0:T(8,128)(2,1)}) custom-call(bf16[128,1024]{1,0:T(8,128)(2,1)} %get-tuple-element.8.att_in, bf16[128,1024]{1,0:T(8,128)(2,1)} %get-tuple-element.9.dq_in, f32[2,128,128]{2,1,0:T(8,128)} %get-tuple-element.10.sums_in, ...), custom_call_target="tpu_custom_call" | custom-call | tf_op jit(solution)/shard_map/pallas_call | solution.py:653

commit v4 on v3

--- a/solution.py
+++ b/solution.py
@@ -71,39 +71,15 @@
         copy.start()
 
     barrier = pltpu.get_barrier_semaphore()
-    for dev in ({"ctx": mate}, ahead, behind):
+    for dev in ({"ctx": mate}, behind):
         pl.semaphore_signal(barrier, inc=1, device_id=dev, device_id_type=MESH)
-    count = 3
+    count = 2
     for d in range(1, 5):
-        up, down = c + 4 * d < n_ctx, c - 4 * d >= 0
-        count = count + up.astype(jnp.int32) + down.astype(jnp.int32)
-
-        @pl.when(up)
-        def _():
-            pl.semaphore_signal(barrier, inc=1, device_id={"ctx": c + 4 * d}, device_id_type=MESH)
-
-        @pl.when(down)
+        count = count + (c + 4 * d < n_ctx).astype(jnp.int32)
+
+        @pl.when(c - 4 * d >= 0)
         def _():
             pl.semaphore_signal(barrier, inc=1, device_id={"ctx": c - 4 * d}, device_id_type=MESH)
-
-    for copy in q_in + g_in:
-        copy.start()
-
-    for i in range(1, PAIRS):
-
-        @pl.when(c < 2 * i)
-        def _():
-            kv[i] = jnp.zeros((2, 2 * T, D), BF16)
-
-    for d in range(1, 5):
-
-        @pl.when(c + 4 * d >= n_ctx)
-        def _():
-            r2[d] = jnp.zeros((2, D, T), BF16)
-
-        @pl.when((c + 4 * d >= n_ctx) | (2 * d - 1 + 2 * z >= PAIRS))
-        def _():
-            r3[d] = jnp.zeros((2, D, T), BF16)
 
     for copy in own_in:
         copy.wait()
@@ -165,6 +141,24 @@
         near_forward(0, kind).start()
 
     start_sends(0)
+    for copy in q_in + g_in:
+        copy.start()
+
+    for i in range(1, PAIRS):
+
+        @pl.when(c < 2 * i)
+        def _():
+            kv[i] = jnp.zeros((2, 2 * T, D), BF16)
+
+    for d in range(1, 5):
+
+        @pl.when(c + 4 * d >= n_ctx)
+        def _():
+            r2[d] = jnp.zeros((2, D, T), BF16)
+
+        @pl.when((c + 4 * d >= n_ctx) | (2 * d - 1 + 2 * z >= PAIRS))
+        def _():
+            r3[d] = jnp.zeros((2, D, T), BF16)
 
     row = c * T + lax.broadcasted_iota(jnp.int32, (T, 2 * T), 0)
     lane = lax.broadcasted_iota(jnp.int32, (T, 2 * T), 1)
@@ -232,8 +226,11 @@
         def _():
             far_forward(i, kind).wait_recv()
 
+    def near_pair(n):
+        return jnp.where(n < 2, 2 * n, 12 - 2 * n)
+
     def near_scores(n, _):
-        i = 2 * n
+        i = near_pair(n)
 
         @pl.when(n == 1)
         def _():
@@ -242,7 +239,7 @@
 
         @pl.when(n < 4)
         def _():
-            take_near(i + 2, 0)
+            take_near(near_pair(n + 1), 0)
 
         await_near(i, 0)
         scores(i, m1)
@@ -255,13 +252,13 @@
         qt[:, rows] = qs[rows].T
 
     def near_weigh(n, _):
-        i = 2 * n
+        i = near_pair(n)
 
         @pl.when(n < 4)
         def _():
-            take_near(i + 2, 1)
-
-        @pl.when(n == 2)
+            take_near(near_pair(n + 1), 1)
+
+        @pl.when(n == 1)
         def _():
             pass_along(1)
 
@@ -278,9 +275,9 @@
         l1[rows] = spread(jnp.sum(l1[rows], axis=1, keepdims=True))
     whole(gs, ld_g).wait()
 
-    for kind in range(2):
+    def cross(kind):
         far_arrived(here, kind).wait_recv()
-        for d in range(1, 5):
+        for d in (2, 1, 3, 4):
 
             @pl.when(relays(d))
             def _():
@@ -289,19 +286,30 @@
         @pl.when(z == 1)
         def _():
             far_forward(1, kind).start()
+
+    cross(0)
 
     @pl.when(z == 0)
     def _():
         take_far(1, 0)
 
-    take_far(3, 0)
+    def far_arrival(n):
+        up = jnp.where(n == 0, 1, 9 - 2 * n)
+        down = jnp.where(n == 0, 1, jnp.where(n == 1, 3, 11 - 2 * n))
+        return jnp.where(z == 0, up, down)
+
+    take_far(far_arrival(1), 0)
 
     def far_scores(n, _):
-        i = 2 * n + 1
+        i = far_arrival(n)
 
         @pl.when(n < 2)
         def _():
-            take_far(i + 4, 0)
+            take_far(far_arrival(n + 2), 0)
+
+        @pl.when(n == 1)
+        def _():
+            cross(1)
 
         await_far(i, 0)
         scores(i, m2)
@@ -313,8 +321,8 @@
     def _():
         take_far(1, 1)
 
-    for i in (3, 5, 7):
-        take_far(i, 1)
+    for n in (1, 2, 3):
+        take_far(far_arrival(n), 1)
 
     for h in range(G):
         rows = pl.ds(h * T, T)
@@ -446,9 +454,9 @@
 
     def attend(t, _):
         rows = pl.ds(pl.multiple_of(t * CHUNK, CHUNK), CHUNK)
-        total = acc[rows] * m1[rows]
-        for i in (1, 3, 5, 7):
-            total = total + dot(pbuf[i, rows], kv[i, 1], NN)
+        weights = jnp.concatenate([pbuf[i, rows] for i in (1, 3, 5, 7)], axis=1)
+        values = jnp.concatenate([kv[i, 1] for i in (1, 3, 5, 7)], axis=0)
+        total = acc[rows] * m1[rows] + dot(weights, values, NN)
         inverse = l2[rows]
         out = (total * inverse).astype(BF16)
         att[rows] = out
@@ -507,7 +515,7 @@
         def _():
             near_swap(i).start()
 
-        @pl.when(n == 1)
+        @pl.when(n == 0)
         def _():
             relay_back(1)
 
@@ -526,9 +534,9 @@
 
     def query_grads(t, _):
         rows = pl.ds(pl.multiple_of(t * CHUNK, CHUNK), CHUNK)
-        total = dot(dsb[0, rows], kv[0, 0], NN)
-        for i in range(1, PAIRS):
-            total = total + dot(dsb[i, rows], kv[i, 0], NN)
+        grads = jnp.concatenate([dsb[i, rows] for i in range(PAIRS)], axis=1)
+        keys = jnp.concatenate([kv[i, 0] for i in range(PAIRS)], axis=0)
+        total = dot(grads, keys, NN)
         dqo[rows] = (total * SCALE).astype(BF16)
         return 0
 

time: 55.1 us -> 57.2 us (1.038)
  Pallas kernels: 54.2 us -> 56.1 us
    pallas_call x1, Pallas kernels: 52.3 us -> 54.1 us  [on_device(): pl.pallas_call(functools.partial(kernel, n_ctx), out_shape=(wide, wide, j...]
where the time goes in v4:
time: 57.2 us; the launch traced here: 56.7 us
  Pallas kernels  56.1 us (98%)
  between operations  0.64 us (1%)
    pallas_call x1, Pallas kernels, on_device(): pl.pallas_call(functools.partial(kernel, n_ctx), out_shape=(wide, wide, j...  54.1 us
    pallas_call x1, Pallas kernels, on_device(): pl.pallas_call(finish, out_shape=(wide, wide, narrow, narrow), in_specs=[...  1.93 us

profile of v4, /device:TPU:6, one launch (start us, length us, event | category | flops | bytes accessed | tf_op | source)
XLA Modules:
  0.0 56.7 jit_solution(9483751075591952259)
XLA Ops:
  0.6 54.1 %shard_map.84 = (bf16[128,1024]{1,0:T(8,128)(2,1)}, bf16[128,1024]{1,0:T(8,128)(2,1)}, f32[2,128,128]{2,1,0:T(8,128)}, bf16[2,128,128]{2,1,0:T(8,128)(2,1)}) custom-call(bf16[128,1024]{1,0:T(8,128)(2,1)} %q_hbm.1, bf16[128,128]{1,0:T(8,128)(2,1)} %k_hbm.1, bf16[128,128]{1,0:T(8,128)(2,1)} %v_hbm.1, bf16[128,1024]{1,0:T(8,128)(2,1)} %g_hbm.1, s32[16]{0:T(128)} %lengths.1), custom_call_target="tpu_custom_call" | custom-call | tf_op jit(solution)/shard_map/pallas_call | solution.py:622
  54.8 1.9 %shard_map.85 = (bf16[128,1024]{1,0:T(8,128)(2,1)}, bf16[128,1024]{1,0:T(8,128)(2,1)}, bf16[128,128]{1,0:T(8,128)(2,1)}, bf16[128,128]{1,0:T(8,128)(2,1)}) custom-call(bf16[128,1024]{1,0:T(8,128)(2,1)} %get-tuple-element.8.att_in, bf16[128,1024]{1,0:T(8,128)(2,1)} %get-tuple-element.9.dq_in, f32[2,128,128]{2,1,0:T(8,128)} %get-tuple-element.10.sums_in, ...), custom_call_target="tpu_custom_call" | custom-call | tf_op jit(solution)/shard_map/pallas_call | solution.py:661

commit v5 on v4

--- a/solution.py
+++ b/solution.py
@@ -275,7 +275,7 @@
         l1[rows] = spread(jnp.sum(l1[rows], axis=1, keepdims=True))
     whole(gs, ld_g).wait()
 
-    def cross(kind):
+    for kind in range(2):
         far_arrived(here, kind).wait_recv()
         for d in (2, 1, 3, 4):
 
@@ -286,8 +286,6 @@
         @pl.when(z == 1)
         def _():
             far_forward(1, kind).start()
-
-    cross(0)
 
     @pl.when(z == 0)
     def _():
@@ -306,10 +304,6 @@
         @pl.when(n < 2)
         def _():
             take_far(far_arrival(n + 2), 0)
-
-        @pl.when(n == 1)
-        def _():
-            cross(1)
 
         await_far(i, 0)
         scores(i, m2)

time: 57.2 us -> 54.7 us (0.956)
  Pallas kernels: 56.1 us -> 53.7 us
    pallas_call x1, Pallas kernels: 54.1 us -> 51.8 us  [on_device(): pl.pallas_call(functools.partial(kernel, n_ctx), out_shape=(wide, wide, j...]
where the time goes in v5:
time: 54.7 us; the launch traced here: 54.3 us
  Pallas kernels  53.7 us (98%)
  between operations  0.64 us (1%)
    pallas_call x1, Pallas kernels, on_device(): pl.pallas_call(functools.partial(kernel, n_ctx), out_shape=(wide, wide, j...  51.8 us
    pallas_call x1, Pallas kernels, on_device(): pl.pallas_call(finish, out_shape=(wide, wide, narrow, narrow), in_specs=[...  1.93 us

profile of v5, /device:TPU:6, one launch (start us, length us, event | category | flops | bytes accessed | tf_op | source)
XLA Modules:
  0.0 54.3 jit_solution(12825463115606836139)
XLA Ops:
  0.6 51.8 %shard_map.84 = (bf16[128,1024]{1,0:T(8,128)(2,1)}, bf16[128,1024]{1,0:T(8,128)(2,1)}, f32[2,128,128]{2,1,0:T(8,128)}, bf16[2,128,128]{2,1,0:T(8,128)(2,1)}) custom-call(bf16[128,1024]{1,0:T(8,128)(2,1)} %q_hbm.1, bf16[128,128]{1,0:T(8,128)(2,1)} %k_hbm.1, bf16[128,128]{1,0:T(8,128)(2,1)} %v_hbm.1, bf16[128,1024]{1,0:T(8,128)(2,1)} %g_hbm.1, s32[16]{0:T(128)} %lengths.1), custom_call_target="tpu_custom_call" | custom-call | tf_op jit(solution)/shard_map/pallas_call | solution.py:616
  52.4 1.9 %shard_map.85 = (bf16[128,1024]{1,0:T(8,128)(2,1)}, bf16[128,1024]{1,0:T(8,128)(2,1)}, bf16[128,128]{1,0:T(8,128)(2,1)}, bf16[128,128]{1,0:T(8,128)(2,1)}) custom-call(bf16[128,1024]{1,0:T(8,128)(2,1)} %get-tuple-element.8.att_in, bf16[128,1024]{1,0:T(8,128)(2,1)} %get-tuple-element.9.dq_in, f32[2,128,128]{2,1,0:T(8,128)} %get-tuple-element.10.sums_in, ...), custom_call_target="tpu_custom_call" | custom-call | tf_op jit(solution)/shard_map/pallas_call | solution.py:655

commit v6 on v5

--- a/solution.py
+++ b/solution.py
@@ -500,8 +500,11 @@
     pass_far(far_pair(2), 0)
     pass_far(far_pair(3), 0)
 
+    def near_order(n):
+        return jnp.where(n < 3, 4 + 2 * n, 8 - 2 * n)
+
     def near(n, _):
-        i = 8 - 2 * n
+        i = near_order(n)
         keep(i, 1, dot(gt[...], pbuf[i], NN))
         score_grads(i, gs, l1, keep)
 
@@ -515,7 +518,7 @@
 
         @pl.when(n > 1)
         def _():
-            pass_near(i + 4)
+            pass_near(near_order(n - 2))
 
         @pl.when(n == 2)
         def _():

time: 54.7 us -> 54.7 us (level)
  no operation moved by 1% of the time
where the time goes in v6:
time: 54.7 us; the launch traced here: 54.3 us
  Pallas kernels  53.7 us (98%)
  between operations  0.64 us (1%)
    pallas_call x1, Pallas kernels, on_device(): pl.pallas_call(functools.partial(kernel, n_ctx), out_shape=(wide, wide, j...  51.8 us
    pallas_call x1, Pallas kernels, on_device(): pl.pallas_call(finish, out_shape=(wide, wide, narrow, narrow), in_specs=[...  1.93 us

profile of v6, /device:TPU:6, one launch (start us, length us, event | category | flops | bytes accessed | tf_op | source)
XLA Modules:
  0.0 54.3 jit_solution(10866756549640683057)
XLA Ops:
  0.6 51.8 %shard_map.84 = (bf16[128,1024]{1,0:T(8,128)(2,1)}, bf16[128,1024]{1,0:T(8,128)(2,1)}, f32[2,128,128]{2,1,0:T(8,128)}, bf16[2,128,128]{2,1,0:T(8,128)(2,1)}) custom-call(bf16[128,1024]{1,0:T(8,128)(2,1)} %q_hbm.1, bf16[128,128]{1,0:T(8,128)(2,1)} %k_hbm.1, bf16[128,128]{1,0:T(8,128)(2,1)} %v_hbm.1, bf16[128,1024]{1,0:T(8,128)(2,1)} %g_hbm.1, s32[16]{0:T(128)} %lengths.1), custom_call_target="tpu_custom_call" | custom-call | tf_op jit(solution)/shard_map/pallas_call | solution.py:619
  52.4 1.9 %shard_map.85 = (bf16[128,1024]{1,0:T(8,128)(2,1)}, bf16[128,1024]{1,0:T(8,128)(2,1)}, bf16[128,128]{1,0:T(8,128)(2,1)}, bf16[128,128]{1,0:T(8,128)(2,1)}) custom-call(bf16[128,1024]{1,0:T(8,128)(2,1)} %get-tuple-element.8.att_in, bf16[128,1024]{1,0:T(8,128)(2,1)} %get-tuple-element.9.dq_in, f32[2,128,128]{2,1,0:T(8,128)} %get-tuple-element.10.sums_in, ...), custom_call_target="tpu_custom_call" | custom-call | tf_op jit(solution)/shard_map/pallas_call | solution.py:658
